TPU v7x, 32 devices: a whole 2x2x4 slice. The times are simulated.
32 devices in a mesh: dp: 8 (over z, core), tensor: 4 (over y, x).
Axes of the slice: x: 2, y: 2, z: 4, core: 2. Of those that a mesh axis runs over, the one named last changes fastest.
Arguments:
- tokens: bfloat16 [10752, 2048], P(('dp', 'tensor')), may hold values from -6 to 6
- segment: int32 [10752], P('dp'), may hold values from 0 to 31, never falling along the last dimension, each value on 1 to 1344 neighbouring positions
- cotangent: bfloat16 [10752, 2048], P(('dp', 'tensor')), may hold values from -6 to 6
- ln1_gain: float32 [2048], replicated, may hold values from 0.1 to 1.9
- ln1_shift: float32 [2048], replicated, may hold values from -3 to 3
- w_query: float32 [2048, 2048], P('dp', 'tensor'), may hold values from -0.125 to 0.125
- b_query: float32 [2048], P('tensor'), may hold values from -3 to 3
- w_keyval: float32 [2048, 256], P(('dp', 'tensor')), may hold values from -0.125 to 0.125
- b_value: float32 [128], replicated, may hold values from -3 to 3
- w_out: float32 [2048, 2048], P('tensor', 'dp'), may hold values from -1 to 1
- b_out: float32 [2048], replicated, may hold values from -3 to 3
- ln2_gain: float32 [2048], replicated, may hold values from 0.1 to 1.9
- ln2_shift: float32 [2048], replicated, may hold values from -3 to 3
- w_in: float32 [2048, 8192], P('dp', 'tensor'), may hold values from -0.125 to 0.125
- b_in: float32 [8192], P('tensor'), may hold values from -3 to 3
- w_back: float32 [8192, 2048], P('tensor', 'dp'), may hold values from -0.0625 to 0.0625
- b_back: float32 [2048], replicated, may hold values from -3 to 3
Outputs:
- output: bfloat16 [10752, 2048], P(('dp', 'tensor'))
- tokens_grad: bfloat16 [10752, 2048], P(('dp', 'tensor'))
- ln1_gain_grad: float32 [2048], P(('dp', 'tensor'))
- ln1_shift_grad: float32 [2048], P(('dp', 'tensor'))
- w_query_grad: float32 [2048, 2048], P('dp', 'tensor')
- b_query_grad: float32 [2048], P('tensor')
- w_keyval_grad: float32 [2048, 256], P(('dp', 'tensor'))
- b_value_grad: float32 [128], P(('dp', 'tensor'))
- w_out_grad: float32 [2048, 2048], P('tensor', 'dp')
- b_out_grad: float32 [2048], P(('dp', 'tensor'))
- ln2_gain_grad: float32 [2048], P(('dp', 'tensor'))
- ln2_shift_grad: float32 [2048], P(('dp', 'tensor'))
- w_in_grad: float32 [2048, 8192], P('dp', 'tensor')
- b_in_grad: float32 [8192], P('tensor')
- w_back_grad: float32 [8192, 2048], P('tensor', 'dp')
- b_back_grad: float32 [2048], P(('dp', 'tensor'))
Inputs may be any that keep to these rules, and one draw needn't show every extreme that they name: `segment`: document numbers never decrease along the tokens; a document has 1 to 1344 tokens and one has exactly 1344.
All inputs are finite; a program needn't handle non-finite values.
Results may differ from a plain program's by a relative error of at most 0.02.
Values may be sent and summed in bfloat16 or wider, within the bound.
A program may use at most 256 MiB of HBM per device.

v0:
```python
import math

import jax
import jax.numpy as jnp
from jax import lax
from jax.sharding import PartitionSpec as P

LEN = 1344


def layer_norm(inputs, norm_gain, norm_shift):
    average = jnp.mean(inputs, axis=-1, keepdims=True)
    centered = inputs - average
    variance = jnp.mean(centered * centered, axis=-1, keepdims=True)
    return centered * lax.rsqrt(variance + 1e-05) * norm_gain + norm_shift


def gelu_tanh(values):
    return jax.nn.gelu(values, approximate=True)


def masked_scores(queries, keys_seq, seg_ids):
    length = seg_ids.shape[0]
    scores = jnp.einsum("qhd,kd->hqk", queries, keys_seq, preferred_element_type=jnp.float32) * (
        1.0 / math.sqrt(keys_seq.shape[1])
    )
    places = jnp.arange(length, dtype=jnp.int32)
    allowed = (seg_ids[:, None] == seg_ids[None, :]) & (places[:, None] >= places[None, :])
    return jnp.where(allowed[None], scores, -1e30)


def attend_forward(inputs):
    queries, keys_seq, values_seq, seg_ids = inputs
    scores = masked_scores(queries, keys_seq, seg_ids)
    largest = jnp.max(scores, axis=-1, keepdims=True)
    exponent = jnp.exp(scores - largest)
    totals = jnp.sum(exponent, axis=-1, keepdims=True)
    weights = (exponent / totals).astype(jnp.bfloat16)
    mixture = jnp.einsum(
        "hqk,kd->qhd", weights, values_seq, preferred_element_type=jnp.float32
    ).astype(jnp.bfloat16)
    return (mixture, largest[..., 0] + jnp.log(totals[..., 0]))


def attend_backward(inputs):
    queries, keys_seq, values_seq, seg_ids, log_total, grad_mix = inputs
    scores = masked_scores(queries, keys_seq, seg_ids)
    probs = jnp.exp(scores - log_total[..., None])
    grad_probs = jnp.einsum("qhd,kd->hqk", grad_mix, values_seq, preferred_element_type=jnp.float32)
    grad_values = jnp.einsum(
        "hqk,qhd->kd", probs.astype(jnp.bfloat16), grad_mix, preferred_element_type=jnp.float32
    )
    inner_sum = jnp.sum(probs * grad_probs, axis=-1, keepdims=True)
    grad_scores = (probs * (grad_probs - inner_sum)).astype(jnp.bfloat16)
    factor = 1.0 / math.sqrt(keys_seq.shape[1])
    grad_queries = (
        jnp.einsum("hqk,kd->qhd", grad_scores, keys_seq, preferred_element_type=jnp.float32)
        * factor
    )
    grad_keys = (
        jnp.einsum("hqk,qhd->kd", grad_scores, queries, preferred_element_type=jnp.float32) * factor
    )
    return (grad_queries, grad_keys, grad_values)


def per_device(
    tokens,
    segment,
    cotangent,
    ln1_gain,
    ln1_shift,
    w_query,
    b_query,
    w_keyval,
    b_value,
    w_out,
    b_out,
    ln2_gain,
    ln2_shift,
    w_in,
    b_in,
    w_back,
    b_back,
):
    inputs = tokens.astype(jnp.float32)
    query_full, inner_full, output_full, down_full = (
        lax.all_gather(w_query.astype(jnp.bfloat16), "dp", axis=0, tiled=True),
        lax.all_gather(w_in.astype(jnp.bfloat16), "dp", axis=0, tiled=True),
        lax.all_gather(w_out.astype(jnp.bfloat16), "dp", axis=1, tiled=True),
        lax.all_gather(w_back.astype(jnp.bfloat16), "dp", axis=1, tiled=True),
    )
    keyval_full = lax.all_gather(
        w_keyval.astype(jnp.bfloat16), ("dp", "tensor"), axis=0, tiled=True
    )
    normed_one, norm_pull_one = jax.vjp(layer_norm, inputs, ln1_gain, ln1_shift)
    normed_low = normed_one.astype(jnp.bfloat16)
    normed_all = lax.all_gather(normed_low, "tensor", axis=0, tiled=True)
    group_rows = normed_all.shape[0]
    head_size = b_value.shape[0]
    local_heads = b_query.shape[0] // head_size
    seq_count = group_rows // LEN
    queries = (
        jnp.dot(normed_all, query_full, preferred_element_type=jnp.float32) + b_query
    ).astype(jnp.bfloat16)
    keyval = jnp.dot(normed_all, keyval_full, preferred_element_type=jnp.float32)
    keys_all = keyval[:, :head_size].astype(jnp.bfloat16)
    values_all = (keyval[:, head_size:] + b_value).astype(jnp.bfloat16)
    query_seq = queries.reshape(seq_count, LEN, local_heads, head_size)
    key_seq = keys_all.reshape(seq_count, LEN, head_size)
    value_seq = values_all.reshape(seq_count, LEN, head_size)
    seg_seq = segment.reshape(seq_count, LEN)
    mixture, log_total = lax.map(attend_forward, (query_seq, key_seq, value_seq, seg_seq))
    mixture = mixture.reshape(group_rows, local_heads * head_size)
    attended = lax.psum_scatter(
        jnp.dot(mixture, output_full, preferred_element_type=jnp.float32).astype(jnp.bfloat16),
        "tensor",
        scatter_dimension=0,
        tiled=True,
    ).astype(jnp.float32)
    hidden = inputs + attended + b_out
    normed_two, norm_pull_two = jax.vjp(layer_norm, hidden, ln2_gain, ln2_shift)
    second_all = lax.all_gather(normed_two.astype(jnp.bfloat16), "tensor", axis=0, tiled=True)
    pre_gelu = jnp.dot(second_all, inner_full, preferred_element_type=jnp.float32) + b_in
    activated, gelu_pull = jax.vjp(gelu_tanh, pre_gelu)
    activated_low = activated.astype(jnp.bfloat16)
    feed_out = lax.psum_scatter(
        jnp.dot(activated_low, down_full, preferred_element_type=jnp.float32).astype(jnp.bfloat16),
        "tensor",
        scatter_dimension=0,
        tiled=True,
    ).astype(jnp.float32)
    output = (hidden + feed_out + b_back).astype(jnp.bfloat16)
    query_again, inner_again, output_again, down_again = (
        lax.all_gather(w_query.astype(jnp.bfloat16), "dp", axis=0, tiled=True),
        lax.all_gather(w_in.astype(jnp.bfloat16), "dp", axis=0, tiled=True),
        lax.all_gather(w_out.astype(jnp.bfloat16), "dp", axis=1, tiled=True),
        lax.all_gather(w_back.astype(jnp.bfloat16), "dp", axis=1, tiled=True),
    )
    grad_out = cotangent.astype(jnp.float32)
    cotangent_all = lax.all_gather(cotangent, "tensor", axis=0, tiled=True)
    down_grad = jnp.einsum(
        "tf,td->fd", activated_low, cotangent_all, preferred_element_type=jnp.float32
    )
    act_grad = jnp.einsum(
        "td,fd->tf", cotangent_all, down_again, preferred_element_type=jnp.float32
    )
    pre_grad = gelu_pull(act_grad)[0].astype(jnp.bfloat16)
    inner_bias_grad = jnp.sum(pre_grad, axis=0, dtype=jnp.float32)
    inner_grad = jnp.einsum("td,tf->df", second_all, pre_grad, preferred_element_type=jnp.float32)
    second_grad = lax.psum_scatter(
        jnp.einsum("tf,df->td", pre_grad, inner_again, preferred_element_type=jnp.float32).astype(
            jnp.bfloat16
        ),
        "tensor",
        scatter_dimension=0,
        tiled=True,
    ).astype(jnp.float32)
    hidden_norm_grad, gain_two_grad, shift_two_grad = norm_pull_two(second_grad)
    hidden_grad = grad_out + hidden_norm_grad
    hidden_all = lax.all_gather(hidden_grad.astype(jnp.bfloat16), "tensor", axis=0, tiled=True)
    output_grad = jnp.einsum("tc,td->cd", mixture, hidden_all, preferred_element_type=jnp.float32)
    mixture_grad = jnp.einsum(
        "td,cd->tc", hidden_all, output_again, preferred_element_type=jnp.float32
    ).astype(jnp.bfloat16)
    query_grads, key_grads, value_grads = lax.map(
        attend_backward,
        (
            query_seq,
            key_seq,
            value_seq,
            seg_seq,
            log_total,
            mixture_grad.reshape(seq_count, LEN, local_heads, head_size),
        ),
    )
    query_low = query_grads.reshape(group_rows, local_heads * head_size).astype(jnp.bfloat16)
    query_bias_grad = jnp.sum(query_low, axis=0, dtype=jnp.float32)
    query_grad = jnp.einsum("td,tc->dc", normed_all, query_low, preferred_element_type=jnp.float32)
    keyval_part = jnp.concatenate(
        [key_grads.reshape(group_rows, head_size), value_grads.reshape(group_rows, head_size)],
        axis=1,
    )
    normed_part = jnp.einsum(
        "tc,dc->td", query_low, query_again, preferred_element_type=jnp.float32
    )
    normed_own, keyval_own = (
        lax.psum_scatter(
            normed_part.astype(jnp.bfloat16), "tensor", scatter_dimension=0, tiled=True
        ).astype(jnp.float32),
        lax.psum_scatter(
            keyval_part.astype(jnp.bfloat16), "tensor", scatter_dimension=0, tiled=True
        ).astype(jnp.float32),
    )
    keyval_low = keyval_own.astype(jnp.bfloat16)
    value_bias_grad = jnp.sum(keyval_low[:, head_size:], axis=0, dtype=jnp.float32)
    keyval_grad = jnp.einsum(
        "td,tc->dc", normed_low, keyval_low, preferred_element_type=jnp.float32
    )
    normed_grad = normed_own + jnp.einsum(
        "tc,dc->td", keyval_low, keyval_full, preferred_element_type=jnp.float32
    )
    input_norm_grad, gain_one_grad, shift_one_grad = norm_pull_one(normed_grad)
    tokens_grad = (hidden_grad + input_norm_grad).astype(jnp.bfloat16)
    out_bias_grad = jnp.sum(hidden_grad, axis=0)
    back_bias_grad = jnp.sum(grad_out, axis=0)
    query_total, inner_total, output_total, down_total = (
        lax.psum_scatter(
            query_grad.astype(jnp.bfloat16), "dp", scatter_dimension=0, tiled=True
        ).astype(jnp.float32),
        lax.psum_scatter(
            inner_grad.astype(jnp.bfloat16), "dp", scatter_dimension=0, tiled=True
        ).astype(jnp.float32),
        lax.psum_scatter(
            output_grad.astype(jnp.bfloat16), "dp", scatter_dimension=1, tiled=True
        ).astype(jnp.float32),
        lax.psum_scatter(
            down_grad.astype(jnp.bfloat16), "dp", scatter_dimension=1, tiled=True
        ).astype(jnp.float32),
    )
    query_bias_total, inner_bias_total = lax.psum((query_bias_grad, inner_bias_grad), "dp")
    shared_total = (
        lax.psum_scatter(keyval_grad, ("dp", "tensor"), scatter_dimension=0, tiled=True),
        lax.psum_scatter(gain_one_grad, ("dp", "tensor"), scatter_dimension=0, tiled=True),
        lax.psum_scatter(shift_one_grad, ("dp", "tensor"), scatter_dimension=0, tiled=True),
        lax.psum_scatter(value_bias_grad, ("dp", "tensor"), scatter_dimension=0, tiled=True),
        lax.psum_scatter(out_bias_grad, ("dp", "tensor"), scatter_dimension=0, tiled=True),
        lax.psum_scatter(gain_two_grad, ("dp", "tensor"), scatter_dimension=0, tiled=True),
        lax.psum_scatter(shift_two_grad, ("dp", "tensor"), scatter_dimension=0, tiled=True),
        lax.psum_scatter(back_bias_grad, ("dp", "tensor"), scatter_dimension=0, tiled=True),
    )
    (
        keyval_total,
        gain_one_total,
        shift_one_total,
        value_bias_total,
        out_bias_total,
        gain_two_total,
        shift_two_total,
        back_bias_total,
    ) = shared_total
    return (
        output,
        tokens_grad,
        gain_one_total,
        shift_one_total,
        query_total,
        query_bias_total,
        keyval_total,
        value_bias_total,
        output_total,
        out_bias_total,
        gain_two_total,
        shift_two_total,
        inner_total,
        inner_bias_total,
        down_total,
        back_bias_total,
    )


def solution(mesh):
    return jax.shard_map(
        per_device,
        mesh=mesh,
        in_specs=(
            P(("dp", "tensor"), None),
            P("dp"),
            P(("dp", "tensor"), None),
            P(),
            P(),
            P("dp", "tensor"),
            P("tensor"),
            P(("dp", "tensor"), None),
            P(),
            P("tensor", "dp"),
            P(),
            P(),
            P(),
            P("dp", "tensor"),
            P("tensor"),
            P("tensor", "dp"),
            P(),
        ),
        out_specs=(
            P(("dp", "tensor"), None),
            P(("dp", "tensor"), None),
            P(("dp", "tensor")),
            P(("dp", "tensor")),
            P("dp", "tensor"),
            P("tensor"),
            P(("dp", "tensor"), None),
            P(("dp", "tensor")),
            P("tensor", "dp"),
            P(("dp", "tensor")),
            P(("dp", "tensor")),
            P(("dp", "tensor")),
            P("dp", "tensor"),
            P("tensor"),
            P("tensor", "dp"),
            P(("dp", "tensor")),
        ),
        check_vma=False,
    )
```

profile of v0, /device:TPU:0, one launch (start us, length us, event | category | flops | bytes accessed | tf_op | source)
XLA Modules:
  0.0 1399.1 jit_solution(5663196500098270768)
XLA Ops:
  7.3 1.6 convert_element_type.150
  8.9 1.6 convert_reduce_fusion.2
  10.5 1.9 fusion.31
  13.1 1.7 fusion.28
  16.5 2.1 fusion.15
  18.5 49.5 %all-gather.12.cloned.1.call-done = bf16[2048,256]{1,0:T(8,128)(2,1)} async-done(((bf16[64,256]{1,0:T(8,128)(2,1)}), bf16[2048,256]{1,0:T(8,128)(2,1)}) %all-gather.12.cloned.1.call-update) | async-done | bytes 1048592 | tf_op jit(solution)/shard_map/all_gather | solution.py:92
  68.0 64.9 %all-gather.10.cloned.1.call-done = bf16[1344,2048]{1,0:T(8,128)(2,1)} async-done(((bf16[336,2048]{1,0:T(8,128)(2,1)}), bf16[1344,2048]{1,0:T(8,128)(2,1)}) %all-gather.10.cloned.1.call-update) | async-done | bytes 5505040 | tf_op jit(solution)/shard_map/all_gather | solution.py:97
  132.9 5.5 fusion.71
  138.5 25.8 %all-gather.14.cloned.1.call-done = bf16[2048,512]{1,0:T(8,128)(2,1)} async-done(((bf16[256,512]{1,0:T(8,128)(2,1)}), bf16[2048,512]{1,0:T(8,128)(2,1)}) %all-gather.14.cloned.1.call-update) | async-done | bytes 2097168 | tf_op jit(solution)/shard_map/all_gather | solution.py:87
  164.3 6.3 fusion.47
  170.7 13.1 fusion.70
  183.8 12.2 fusion.2
  196.0 14.4 %fusion.35 = bf16[1344,4,128]{2,0,1:T(8,128)(2,1)} fusion(f32[4,1344,1344]{1,2,0:T(8,128)} %get-tuple-element.91, f32[4,1344]{1,0:T(4,128)S(1)} %fusion.2, f32[4,1344]{1,0:T(4,128)S(1)} %get-tuple-element.90, f32[1344,256]{1,0:T(8,128)S(1)} %copy-done.10, f32[128]{0:T(128)S(1)} %copy-done.35), kind=kOutput, calls=%fused_computation.73 | convolution fusion | flops 1872396288 | bytes 31011328 | tf_op jit(solution)/shard_map/while/body/eval_jaxpr/hqk,kd->qhd/dot_general | solution.py:39
  210.4 1.8 copy.49
  212.3 7.6 convolution_convert_fusion.5
  219.9 1.5 copy-done.7
  222.7 60.2 %reduce-scatter.11.cloned.1.call-done = bf16[336,2048]{1,0:T(8,128)(2,1)} async-done(((bf16[1344,2048]{1,0:T(8,128)(2,1)}), bf16[336,2048]{1,0:T(8,128)(2,1)}) %reduce-scatter.11.cloned.1.call-update) | async-done | bytes 1376272 | tf_op jit(solution)/shard_map/reduce_scatter | solution.py:114
  282.9 2.0 fusion.45
  285.7 1.9 add_convert_fusion.2
  288.4 2.7 convert_element_type.163
  291.2 75.3 %all-gather.20.cloned.1.call-done = bf16[2048,2048]{1,0:T(8,128)(2,1)} async-done(((bf16[256,2048]{1,0:T(8,128)(2,1)}), bf16[2048,2048]{1,0:T(8,128)(2,1)}) %all-gather.20.cloned.1.call-update) | async-done | bytes 8388624 | tf_op jit(solution)/shard_map/all_gather | solution.py:88
  366.4 64.4 %all-gather.18.cloned.1.call-done = bf16[1344,2048]{1,0:T(8,128)(2,1)} async-done(((bf16[336,2048]{1,0:T(8,128)(2,1)}), bf16[1344,2048]{1,0:T(8,128)(2,1)}) %all-gather.18.cloned.1.call-update) | async-done | bytes 5505040 | tf_op jit(solution)/shard_map/all_gather | solution.py:122
  430.8 18.4 %fusion.72 = f32[1344,2048]{1,0:T(8,128)} fusion(bf16[1344,2048]{1,0:T(8,128)(2,1)} %all-gather.18.cloned.1.call-done, bf16[2048,2048]{1,0:T(8,128)(2,1)} %all-gather.20.cloned.1.call-done), kind=kOutput, calls=%fused_computation.115 | convolution fusion | flops 11274289152 | bytes 24903680 | tf_op jit(solution)/shard_map/dot_general | solution.py:123
  449.3 46.9 %all-gather.24.cloned.1.call-done = bf16[1344,2048]{1,0:T(8,128)(2,1)} async-done(((bf16[336,2048]{1,0:T(8,128)(2,1)}), bf16[1344,2048]{1,0:T(8,128)(2,1)}) %all-gather.24.cloned.1.call-update) | async-done | bytes 5505040 | tf_op jit(solution)/shard_map/all_gather | solution.py:140
  496.2 84.1 %all-gather.22.cloned.1.call-done = bf16[2048,2048]{1,0:T(8,128)(2,1)} async-done(((bf16[2048,256]{1,0:T(8,128)(2,1)}), bf16[2048,2048]{1,0:T(8,128)(2,1)}) %all-gather.22.cloned.1.call-update) | async-done | bytes 8388624 | tf_op jit(solution)/shard_map/all_gather | solution.py:90
  580.3 24.8 %convert_reduce_fusion = (f32[2048]{0:T(1024)}, bf16[1344,2048]{1,0:T(8,128)(2,1)S(1)}) fusion(f32[1344,2048]{1,0:T(8,128)} %fusion.72, f32[2048]{0:T(1024)S(1)} %copy-done.36, bf16[1344,2048]{1,0:T(8,128)(2,1)} %all-gather.24.cloned.1.call-done, bf16[2048,2048]{1,0:T(8,128)(2,1)} %all-gather.22.cloned.1.call-done), kind=kOutput, calls=%fused_computation.23 | convolution fusion | flops 11337594880 | bytes 30425088 | tf_op jit(solution)/shard_map/td,fd->tf/dot_general | solution.py:144
  605.1 2.4 copy-done.39
  607.5 15.8 %convolution_convert_fusion.3 = bf16[1344,2048]{1,0:T(8,128)(2,1)} fusion(bf16[1344,2048]{1,0:T(8,128)(2,1)S(1)} %get-tuple-element.85, bf16[2048,2048]{1,0:T(8,128)(2,1)} %all-gather.20.cloned.1.call-done), kind=kOutput, calls=%fused_computation.30 | convolution fusion | flops 11277041664 | bytes 19398656 | tf_op jit(solution)/shard_map/tf,df->td/dot_general | solution.py:151
  623.4 19.6 %convolution_convert_fusion.4 = bf16[1344,2048]{1,0:T(8,128)(2,1)} fusion(bf16[2048,2048]{1,0:T(8,128)(2,1)} %all-gather.22.cloned.1.call-done, f32[1344,2048]{1,0:T(8,128)} %fusion.72, f32[2048]{0:T(1024)S(1)} %copy-done.36), kind=kOutput, calls=%fused_computation.31 | convolution fusion | flops 11304566784 | bytes 24911872 | tf_op jit(solution)/shard_map/dot_general | solution.py:127
  643.3 41.9 %reduce-scatter.15.cloned.1.call-done = bf16[336,2048]{1,0:T(8,128)(2,1)} async-done(((bf16[1344,2048]{1,0:T(8,128)(2,1)}), bf16[336,2048]{1,0:T(8,128)(2,1)}) %reduce-scatter.15.cloned.1.call-update) | async-done | bytes 1376272 | tf_op jit(solution)/shard_map/reduce_scatter | solution.py:150
  685.2 3.1 convert_reduce_fusion.1
  688.4 2.2 fusion.34
  690.6 61.2 %reduce-scatter.13.cloned.1.call-done = bf16[336,2048]{1,0:T(8,128)(2,1)} async-done(((bf16[1344,2048]{1,0:T(8,128)(2,1)}), bf16[336,2048]{1,0:T(8,128)(2,1)}) %reduce-scatter.13.cloned.1.call-update) | async-done | bytes 1376272 | tf_op jit(solution)/shard_map/reduce_scatter | solution.py:126
  751.8 5.6 fusion.69
  757.3 1.5 copy-done.3
  760.2 63.6 %all-gather.26.cloned.1.call-done = bf16[1344,2048]{1,0:T(8,128)(2,1)} async-done(((bf16[336,2048]{1,0:T(8,128)(2,1)}), bf16[1344,2048]{1,0:T(8,128)(2,1)}) %all-gather.26.cloned.1.call-update) | async-done | bytes 5505040 | tf_op jit(solution)/shard_map/all_gather | solution.py:160
  823.8 6.3 fusion.46
  830.1 15.2 %fusion.41 = bf16[1344,128]{1,0:T(8,128)(2,1)S(1)} fusion(f32[4,1344,1344]{1,2,0:T(8,128)} %get-tuple-element.91, f32[4,1344]{1,0:T(4,128)S(1)} %log_add_fusion, bf16[168,4,8,128]{3,2,1,0:T(8,128)(2,1)S(1)} %fusion.46), kind=kOutput, calls=%fused_computation.78 | convolution fusion | flops 1864310784 | bytes 30643200 | tf_op jit(solution)/shard_map/while/body/eval_jaxpr/hqk,qhd->kd/dot_general | solution.py:50
  845.3 22.9 %multiply_reduce_fusion = (f32[4,1344]{1,0:T(4,128)S(1)}, f32[4,1344,1344]{1,2,0:T(8,128)}) fusion(f32[4,1344,1344]{1,2,0:T(8,128)} %get-tuple-element.91, f32[4,1344]{1,0:T(4,128)S(1)} %log_add_fusion, bf16[168,4,8,128]{3,2,1,0:T(8,128)(2,1)S(1)} %fusion.46, f32[1344,256]{1,0:T(8,128)S(1)} %copy-done.11, f32[128]{0:T(128)S(1)} %copy-done.35), kind=kOutput, calls=%fused_computation.5 | convolution fusion | flops 1871702784 | bytes 59911680 | tf_op jit(solution)/shard_map/while/body/eval_jaxpr/qhd,kd->hqk/dot_general | solution.py:49
  868.2 25.3 %multiply_convert_fusion = bf16[4,1344,1344]{1,2,0:T(8,128)(2,1)} fusion(f32[4,1344,1344]{1,2,0:T(8,128)} %get-tuple-element.93, f32[4,1344,1344]{1,2,0:T(8,128)} %get-tuple-element.91, f32[4,1344]{1,0:T(4,128)S(1)} %get-tuple-element.92, f32[4,1344]{1,0:T(4,128)S(1)} %log_add_fusion), kind=kLoop, calls=%fused_computation.4 | loop fusion | flops 28901376 | bytes 72296448 | tf_op jit(solution)/shard_map/while/body/eval_jaxpr/convert_element_type | solution.py:54
  893.5 9.7 fusion.40
  904.2 22.3 %convolution_convert_fusion = bf16[2048,2048]{1,0:T(8,128)(2,1)} fusion(bf16[1344,2048]{1,0:T(8,128)(2,1)} %all-gather.24.cloned.1.call-done, f32[1344,2048]{1,0:T(8,128)} %fusion.72, f32[2048]{0:T(1024)S(1)} %copy-done.36), kind=kOutput, calls=%fused_computation.27 | convolution fusion | flops 11306008576 | bytes 24911872 | tf_op jit(solution)/shard_map/tf,td->fd/dot_general | solution.py:141
  926.6 19.2 %convolution_convert_fusion.1 = bf16[2048,2048]{1,0:T(8,128)(2,1)} fusion(bf16[1344,2048]{1,0:T(8,128)(2,1)} %all-gather.18.cloned.1.call-done, bf16[1344,2048]{1,0:T(8,128)(2,1)} %copy-done.39), kind=kOutput, calls=%fused_computation.28 | convolution fusion | flops 11278483456 | bytes 19398656 | tf_op jit(solution)/shard_map/td,tf->df/dot_general | solution.py:149
  945.9 1.3 copy-done.9
  947.2 7.2 convolution_convert_fusion.7
  954.8 11.6 convert_reduce_fusion.4
  967.2 7.5 convolution_convert_fusion.8
  974.8 7.4 convolution_convert_fusion.2
  983.5 3.0 fusion.73
  986.6 35.3 %reduce-scatter.29.cloned.1.call-done = bf16[2048,256]{1,0:T(8,128)(2,1)} async-done(((bf16[2048,2048]{1,0:T(8,128)(2,1)}), bf16[2048,256]{1,0:T(8,128)(2,1)}) %reduce-scatter.29.cloned.1.call-update) | async-done | bytes 1048592 | tf_op jit(solution)/shard_map/reduce_scatter | solution.py:216
  1021.8 2.7 convert_element_type.191
  1024.5 87.4 %reduce-scatter.27.cloned.1.call-done = bf16[256,2048]{1,0:T(8,128)(2,1)} async-done(((bf16[2048,2048]{1,0:T(8,128)(2,1)}), bf16[256,2048]{1,0:T(8,128)(2,1)}) %reduce-scatter.27.cloned.1.call-update) | async-done | bytes 1048592 | tf_op jit(solution)/shard_map/reduce_scatter | solution.py:210
  1112.0 2.8 convert_element_type.188
  1114.8 26.2 %all-reduce.8 = (f32[512]{0:T(512)}, f32[2048]{0:T(1024)}) all-reduce(f32[512]{0:T(512)S(1)} %bitcast.91, f32[2048]{0:T(1024)S(1)} %copy-done.33), channel_id=1, replica_groups=mesh['dp'=8,'tensor'=4] {'dp'}, use_global_device_ids=true, to_apply=%region_22.23 | all-reduce | flops 2560 | bytes 20480 | tf_op jit(solution)/shard_map/psum | solution.py:220
  1141.1 7.8 reduce-scatter.25.cloned.1.call-done
  1148.8 1.8 convert_element_type.186
  1150.6 35.1 %reduce-scatter.21.cloned.1.call-done = bf16[256,512]{1,0:T(8,128)(2,1)} async-done(((bf16[2048,512]{1,0:T(8,128)(2,1)}), bf16[256,512]{1,0:T(8,128)(2,1)}) %reduce-scatter.21.cloned.1.call-update) | async-done | bytes 262160 | tf_op jit(solution)/shard_map/reduce_scatter | solution.py:207
  1185.7 1.8 convert_element_type.182
  1187.5 63.3 %reduce-scatter.17.cloned.1.call-done = bf16[336,2048]{1,0:T(8,128)(2,1)} async-done(((bf16[1344,2048]{1,0:T(8,128)(2,1)}), bf16[336,2048]{1,0:T(8,128)(2,1)}) %reduce-scatter.17.cloned.1.call-update) | async-done | bytes 1376272 | tf_op jit(solution)/shard_map/reduce_scatter | solution.py:187
  1250.8 2.4 fusion.67
  1253.2 1.5 copy-done.4
  1256.0 40.4 %all-reduce.7 = (f32[2048]{0:T(1024)S(1)}, f32[2048]{0:T(1024)S(1)}, f32[128]{0:T(128)S(1)}, f32[2048]{0:T(1024)S(1)}, f32[2048]{0:T(1024)S(1)}, /*index=5*/f32[2048]{0:T(1024)S(1)}, f32[2048]{0:T(1024)S(1)}) all-reduce(f32[2048]{0:T(1024)S(1)} %get-tuple-element.69, ...), channel_id=7, replica_groups=mesh['dp'=8,'tensor'=4] {'dp','tensor'}, use_global_device_ids=true, to_apply=%region_17.18.clone | all-reduce | flops 12416 | bytes 99328
  1300.5 4.7 add_convert_fusion
  1305.1 86.9 %reduce-scatter.23.cloned.1.call-done = f32[64,256]{1,0:T(8,128)} async-done(((f32[2048,256]{1,0:T(8,128)}), f32[64,256]{1,0:T(8,128)}) %reduce-scatter.23.cloned.1.call-update) | async-done | bytes 65552 | tf_op jit(solution)/shard_map/reduce_scatter | solution.py:222
  (140 shorter events, 16.1 us)
Async XLA Ops:
  7.2 5.9 copy-start
  7.2 5.9 copy-start.18
  7.2 5.9 copy-start.31
  7.2 60.8 %all-gather.12.cloned.1.call-start = ((), (), s32[]{:S(2)}) async-start(), calls=%async_computation.11 | async-start | bytes 1081344 | tf_op jit(solution)/shard_map/all_gather | solution.py:92
  8.8 124.1 %all-gather.10.cloned.1.call-start = ((), (), s32[]{:S(2)}) async-start(), calls=%async_computation.10 | async-start | bytes 6881280 | tf_op jit(solution)/shard_map/all_gather | solution.py:97
  10.5 2.5 copy-start.20
  10.5 4.3 copy-start.14
  12.4 0.6 copy-start.29
  13.0 2.6 copy-start.15
  13.1 3.3 copy-start.27
  13.1 3.4 copy-start.22
  14.8 149.5 %all-gather.14.cloned.1.call-start = ((), (), s32[]{:S(2)}) async-start(), calls=%async_computation.12 | async-start | bytes 2359296 | tf_op jit(solution)/shard_map/all_gather | solution.py:87
  15.6 196.7 %all-gather.16.cloned.1.call-start = ((), (), s32[]{:S(2)}) async-start(), calls=%async_computation.13 | async-start | bytes 2359296 | tf_op jit(solution)/shard_map/all_gather | solution.py:89
  16.4 266.5 %reduce-scatter.11.cloned.1.call-start = ((), (), s32[]{:S(2)}) async-start(), calls=%async_computation.14 | async-start | bytes 6881280 | tf_op jit(solution)/shard_map/reduce_scatter | solution.py:114
  18.5 145.8 %copy-start.37 = (f32[512]{0:T(512)S(1)}, f32[512]{0:T(512)}, u32[]{:S(2)}) copy-start(f32[512]{0:T(512)} %param.23) | copy-start | bytes 6148
  164.3 6.3 copy-start.10
  170.7 13.1 copy-start.38
  183.8 12.2 copy-start.35
  212.2 7.6 copy-start.8
  219.8 1.6 copy-start.7
  219.9 63.1 %copy-start.16 = (f32[2048]{0:T(1024)S(1)}, f32[2048]{0:T(1024)}, u32[]{:S(2)}) copy-start(f32[2048]{0:T(1024)} %param.27) | copy-start | bytes 24580
  219.9 146.6 %all-gather.20.cloned.1.call-start = ((), (), s32[]{:S(2)}) async-start(), calls=%async_computation.16 | async-start | bytes 9437184 | tf_op jit(solution)/shard_map/all_gather | solution.py:88
  222.6 63.1 %copy-start.17 = (f32[2048]{0:T(1024)S(1)}, f32[2048]{0:T(1024)}, u32[]{:S(2)}) copy-start(f32[2048]{0:T(1024)} %param.28) | copy-start | bytes 24580
  222.6 63.1 %copy-start.32 = (f32[2048]{0:T(1024)S(1)}, f32[2048]{0:T(1024)}, u32[]{:S(2)}) copy-start(f32[2048]{0:T(1024)} %param.29) | copy-start | bytes 24580
  222.6 208.2 %all-gather.18.cloned.1.call-start = ((), (), s32[]{:S(2)}) async-start(), calls=%async_computation.15 | async-start | bytes 6881280 | tf_op jit(solution)/shard_map/all_gather | solution.py:122
  282.9 2.0 copy-start.2
  287.6 208.6 %all-gather.24.cloned.1.call-start = ((), (), s32[]{:S(2)}) async-start(), calls=%async_computation.19 | async-start | bytes 6881280 | tf_op jit(solution)/shard_map/all_gather | solution.py:140
  288.3 292.0 %all-gather.22.cloned.1.call-start = ((), (), s32[]{:S(2)}) async-start(), calls=%async_computation.17 | async-start | bytes 9437184 | tf_op jit(solution)/shard_map/all_gather | solution.py:90
  291.1 289.2 %copy-start.36 = (f32[2048]{0:T(1024)S(1)}, f32[2048]{0:T(1024)}, u32[]{:S(2)}) copy-start(f32[2048]{0:T(1024)} %param.31) | copy-start | bytes 24580
  291.1 394.1 %reduce-scatter.15.cloned.1.call-start = ((), (), s32[]{:S(2)}) async-start(), calls=%async_computation.20 | async-start | bytes 6881280 | tf_op jit(solution)/shard_map/reduce_scatter | solution.py:150
  605.1 2.4 copy-start.39
  623.3 128.4 %reduce-scatter.13.cloned.1.call-start = ((), (), s32[]{:S(2)}) async-start(), calls=%async_computation.18 | async-start | bytes 6881280 | tf_op jit(solution)/shard_map/reduce_scatter | solution.py:126
  643.1 180.7 %all-gather.26.cloned.1.call-start = ((), (), s32[]{:S(2)}) async-start(), calls=%async_computation.21 | async-start | bytes 6881280 | tf_op jit(solution)/shard_map/all_gather | solution.py:160
  685.2 3.1 copy-start.6
  688.3 63.5 %copy-start.34 = (f32[2048]{0:T(1024)S(1)}, f32[2048]{0:T(1024)}, u32[]{:S(2)}) copy-start(f32[2048]{0:T(1024)} %param.33) | copy-start | bytes 24580
  757.3 1.5 copy-start.3
  760.1 222.4 %reduce-scatter.19.cloned.1.call-start = ((), (), s32[]{:S(2)}) async-start(), calls=%async_computation.23 | async-start | bytes 860160 | tf_op jit(solution)/shard_map/reduce_scatter | solution.py:190
  830.1 15.2 %copy-start.11 = (f32[1344,256]{1,0:T(8,128)S(1)}, f32[1344,256]{1,0:T(8,128)}, u32[]{:S(2)}) copy-start(f32[1344,256]{1,0:T(8,128)} %fusion.71) | copy-start | bytes 4128772
  904.1 117.7 %reduce-scatter.29.cloned.1.call-start = ((), (), s32[]{:S(2)}) async-start(), calls=%async_computation.28 | async-start | bytes 9437184 | tf_op jit(solution)/shard_map/reduce_scatter | solution.py:216
  926.5 185.4 %reduce-scatter.27.cloned.1.call-start = ((), (), s32[]{:S(2)}) async-start(), calls=%async_computation.27 | async-start | bytes 9437184 | tf_op jit(solution)/shard_map/reduce_scatter | solution.py:210
  945.8 1.4 copy-start.9
  945.8 203.0 %reduce-scatter.25.cloned.1.call-start = ((), (), s32[]{:S(2)}) async-start(), calls=%async_computation.26 | async-start | bytes 2359296 | tf_op jit(solution)/shard_map/reduce_scatter | solution.py:213
  954.5 231.2 %reduce-scatter.21.cloned.1.call-start = ((), (), s32[]{:S(2)}) async-start(), calls=%async_computation.24 | async-start | bytes 2359296 | tf_op jit(solution)/shard_map/reduce_scatter | solution.py:207
  974.7 276.0 %reduce-scatter.17.cloned.1.call-start = ((), (), s32[]{:S(2)}) async-start(), calls=%async_computation.22 | async-start | bytes 6881280 | tf_op jit(solution)/shard_map/reduce_scatter | solution.py:187
  982.1 1.4 copy-start.5
  982.2 409.9 %reduce-scatter.23.cloned.1.call-start = ((), (), s32[]{:S(2)}) async-start(), calls=%async_computation.25 | async-start | bytes 2162688 | tf_op jit(solution)/shard_map/reduce_scatter | solution.py:222
  986.6 128.2 %copy-start.33 = (f32[2048]{0:T(1024)S(1)}, f32[2048]{0:T(1024)}, u32[]{:S(2)}) copy-start(f32[2048]{0:T(1024)} %get-tuple-element.84) | copy-start | bytes 24580
  986.6 154.4 %copy-start.12 = (bf16[336,256]{1,0:T(8,128)(2,1)S(1)}, bf16[336,256]{1,0:T(8,128)(2,1)}, u32[]{:S(2)}) copy-start(bf16[336,256]{1,0:T(8,128)(2,1)} %reduce-scatter.19.cloned.1.call-done) | copy-start | bytes 516100
  1024.5 226.2 %copy-start.1 = (bf16[336,2048]{1,0:T(8,128)(2,1)S(1)}, bf16[336,2048]{1,0:T(8,128)(2,1)}, u32[]{:S(2)}) copy-start(bf16[336,2048]{1,0:T(8,128)(2,1)} %param.17) | copy-start | bytes 4128772
  1024.5 226.2 %copy-start.13 = (bf16[2048,256]{1,0:T(8,128)(2,1)S(1)}, bf16[2048,256]{1,0:T(8,128)(2,1)}, u32[]{:S(2)}) copy-start(bf16[2048,256]{1,0:T(8,128)(2,1)} %all-gather.12.cloned.1.call-done) | copy-start | bytes 3145732
  1024.5 226.2 %copy-start.19 = (f32[2048]{0:T(1024)S(1)}, f32[2048]{0:T(1024)}, u32[]{:S(2)}) copy-start(f32[2048]{0:T(1024)} %param.20) | copy-start | bytes 24580
  1024.5 226.2 %copy-start.21 = (f32[336]{0:T(512)S(1)}, f32[336]{0:T(512)}, u32[]{:S(2)}) copy-start(f32[336]{0:T(512)} %copy-done.20) | copy-start | bytes 4036
  1187.5 65.8 %copy-start.30 = (f32[336]{0:T(512)S(1)}, f32[336]{0:T(512)}, u32[]{:S(2)}) copy-start(f32[336]{0:T(512)} %copy-done.29) | copy-start | bytes 4036
  1187.5 67.2 %copy-start.28 = (f32[336]{0:T(512)S(1)}, f32[336]{0:T(512)}, u32[]{:S(2)}) copy-start(f32[336]{0:T(512)} %copy-done.27) | copy-start | bytes 4036
  1253.2 1.5 copy-start.4
  1253.2 2.8 copy-start.23
  1253.2 2.8 copy-start.24
  1253.2 2.8 copy-start.25
  1253.2 2.8 copy-start.26
Sparse Core Ops, SparseCore 0:
  11.6 56.3 all-gather.11
  70.4 62.4 all-gather.9
  135.1 29.1 all-gather.13
  166.3 29.9 all-gather.15
  220.0 62.8 reduce-scatter.10
  284.4 82.0 all-gather.19
  368.8 61.9 all-gather.17
  432.7 63.4 all-gather.23
  497.8 82.4 all-gather.21
  623.5 61.6 reduce-scatter.14
  688.3 63.4 reduce-scatter.12
  760.3 63.4 all-gather.25
  904.3 25.8 reduce-scatter.18
  932.3 89.5 reduce-scatter.28
  1024.0 87.9 reduce-scatter.26
  1114.1 34.6 reduce-scatter.24
  1151.0 34.6 reduce-scatter.20
  1188.6 62.1 reduce-scatter.16
  1253.6 138.4 reduce-scatter.22
where the time goes:
time: 1410 us; the launch traced here: 1400 us
  waiting for transfers between devices  955 us (68%)
  matrix products  260 us (18%)
  other arithmetic  84.4 us (6%)
  blocking collectives  66.6 us (5%)
  local copies, waits for them, and re-layouts  16.6 us (1%)
  between operations  15 us (1%)
    reduce_scatter x1, waiting for transfers between devices, per_device(): lax.psum_scatter(inner_grad.astype(jnp.bfloat16), 'dp', scatter_dimension...  87.4 us
    reduce_scatter x1, waiting for transfers between devices, per_device(): lax.psum_scatter(keyval_grad, ('dp', 'tensor'), scatter_dimension=0, tile...  86.9 us
    all_gather x1, waiting for transfers between devices, per_device(): lax.all_gather(w_back.astype(jnp.bfloat16), 'dp', axis=1, tiled=True)  84.1 us
    all_gather x1, waiting for transfers between devices, per_device(): lax.all_gather(w_in.astype(jnp.bfloat16), 'dp', axis=0, tiled=True)  75.3 us
    all_gather x1, waiting for transfers between devices, per_device(): normed_all = lax.all_gather(normed_low, 'tensor', axis=0, tiled=True)  64.9 us
    all_gather x1, waiting for transfers between devices, per_device(): lax.all_gather(normed_two.astype(jnp.bfloat16), 'tensor', axis=0, tiled=T...  64.4 us
    all_gather x1, waiting for transfers between devices, per_device(): lax.all_gather(hidden_grad.astype(jnp.bfloat16), 'tensor', axis=0, tiled=...  63.6 us
    reduce_scatter x1, waiting for transfers between devices, per_device(): lax.psum_scatter(normed_part.astype(jnp.bfloat16), 'tensor', scatter_dime...  63.3 us
  transfers between devices with their start and end apart: 19, of which 17 were waited for; matrix products, arithmetic and copies ran while one was open for 15% of the time, Pallas kernels for 0%

commit v1 on v0

v1 whole, which is shorter than its diff:
```python
import functools
import math

import jax
import jax.numpy as jnp
from jax import lax
from jax.experimental import pallas as pl
from jax.experimental.pallas import tpu as pltpu
from jax.sharding import PartitionSpec as P

LEN = 1344
HD = 128
QB = 112
KB = 224
SCALE = 1.0 / math.sqrt(HD)
EXP2 = SCALE * math.log2(math.e)
NEG = -1e30
BF = jnp.bfloat16
F32 = jnp.float32


def _stack(ref, heads):
    return jnp.concatenate([ref[0, :, h * HD : (h + 1) * HD] for h in range(heads)], axis=0)


def _allowed(info_ref, first):
    shape = (KB, info_ref.shape[2])
    place = lax.broadcasted_iota(jnp.int32, shape, 0) + first
    return (place >= info_ref[0, 0:1, :]) & (place <= info_ref[0, 1:2, :])


def _nt(a, b):
    return lax.dot_general(a, b, (((1,), (1,)), ((), ())), preferred_element_type=F32)


def attend_kernel(heads, place_ref, low_ref, top_ref, q_ref, k_ref, vt_ref, info_ref, o_ref, lse_ref, s_ref):
    step = pl.program_id(0)
    low, top = low_ref[step], top_ref[step]
    q = _stack(q_ref, heads)
    rows = q.shape[0]

    def score(c, best):
        s = _nt(k_ref[0, pl.ds(pl.multiple_of(c * KB, KB), KB), :], q)
        s = jnp.where(_allowed(info_ref, c * KB), s, NEG)
        s_ref[c] = s
        return jnp.maximum(best, jnp.max(s, axis=0, keepdims=True))

    best = lax.fori_loop(low, top, score, jnp.full((1, rows), NEG, F32))
    shift = best * EXP2

    def mix(c, carry):
        total, acc = carry
        p = jnp.exp2(s_ref[c] * EXP2 - shift)
        total = total + jnp.sum(p, axis=0, keepdims=True)
        acc = acc + jnp.dot(vt_ref[0, c], p.astype(BF), preferred_element_type=F32)
        return total, acc

    total, acc = lax.fori_loop(
        low, top, mix, (jnp.zeros((1, rows), F32), jnp.zeros((HD, rows), F32))
    )
    out = (acc / total).T.astype(BF)
    for h in range(heads):
        o_ref[0, :, h * HD : (h + 1) * HD] = out[h * QB : (h + 1) * QB]
    lse_ref[0] = jnp.broadcast_to(shift + jnp.log2(total), lse_ref.shape[1:])


def attend_back_kernel(
    heads, per_seq, place_ref, low_ref, top_ref, q_ref, o_ref, do_ref, k_ref, v_ref, kt_ref, info_ref, lse_ref,
    dq_ref, dkv_ref, dk_acc, dv_acc,
):
    step = pl.program_id(0)
    inner = lax.rem(step, per_seq)
    low, top = low_ref[step], top_ref[step]

    @pl.when(inner == 0)
    def _():
        dk_acc[...] = jnp.zeros_like(dk_acc)
        dv_acc[...] = jnp.zeros_like(dv_acc)

    q = _stack(q_ref, heads)
    do = _stack(do_ref, heads)
    rows = q.shape[0]
    prod = do.astype(F32) * _stack(o_ref, heads).astype(F32)
    delta = jnp.sum(prod.T, axis=0, keepdims=True)
    lse = lse_ref[0, 0:1, :]

    def body(c, acc):
        window = pl.ds(pl.multiple_of(c * KB, KB), KB)
        s = _nt(k_ref[0, window, :], q)
        s = jnp.where(_allowed(info_ref, c * KB), s * EXP2 - lse, NEG)
        p = jnp.exp2(s)
        dp = _nt(v_ref[0, window, :], do)
        ds = (p * (dp - delta)).astype(BF)
        dv_acc[window, :] += jnp.dot(p.astype(BF), do, preferred_element_type=F32)
        dk_acc[window, :] += jnp.dot(ds, q, preferred_element_type=F32)
        return acc + jnp.dot(kt_ref[0, c], ds, preferred_element_type=F32)

    acc = lax.fori_loop(low, top, body, jnp.zeros((HD, rows), F32))
    dq = (acc * SCALE).T.astype(BF)
    for h in range(heads):
        dq_ref[0, :, h * HD : (h + 1) * HD] = dq[h * QB : (h + 1) * QB]

    @pl.when(inner == per_seq - 1)
    def _():
        dkv_ref[0, :, :HD] = (dk_acc[...] * SCALE).astype(BF)
        dkv_ref[0, :, HD:] = dv_acc[...].astype(BF)


class Attention:
    def __init__(self, segment, place, rows, heads):
        self.heads, self.rows = heads, rows
        self.seqs = segment.shape[0] // LEN
        self.per_seq = LEN // QB
        self.per_block = rows // QB
        self.steps = self.seqs * self.per_seq
        self.place = place
        seg = segment.reshape(self.seqs, LEN)
        start = jnp.sum((seg[:, None, :] < seg[:, :, None]).astype(jnp.int32), axis=-1)
        pos = jnp.broadcast_to(jnp.arange(LEN, dtype=jnp.int32), seg.shape)
        info = jnp.stack([start, pos], axis=1).reshape(self.seqs, 2, self.per_seq, 1, QB)
        info = jnp.broadcast_to(info, (self.seqs, 2, self.per_seq, heads, QB))
        self.info = info.transpose(0, 2, 1, 3, 4).reshape(self.steps, 2, heads * QB)
        self.low = start.reshape(self.steps, QB)[:, 0] // KB
        last = pos.reshape(self.steps, QB)[:, -1]
        self.top = last // KB + 1

    def _specs(self):
        per_seq, per_block, heads = self.per_seq, self.per_block, self.heads
        wide = heads * HD
        query = pl.BlockSpec((1, QB, wide), lambda i, place, *_: (place[i // per_block], i % per_block, 0))
        key = pl.BlockSpec((1, LEN, HD), lambda i, *_: (i // per_seq, 0, 0))
        keyt = pl.BlockSpec((1, LEN // KB, HD, KB), lambda i, *_: (i // per_seq, 0, 0, 0))
        info = pl.BlockSpec((1, 2, heads * QB), lambda i, *_: (i, 0, 0))
        lse = pl.BlockSpec((1, 8, heads * QB), lambda i, *_: (i, 0, 0))
        return query, key, keyt, info, lse

    def _cost(self, products):
        pairs = self.steps * QB * self.heads * LEN // 2
        return pl.CostEstimate(
            flops=2 * pairs * HD * products, transcendentals=pairs, bytes_accessed=8 * self.steps * QB * HD * self.heads
        )

    def forward(self, q, keys, values_t):
        query, key, keyt, info, lse = self._specs()
        lanes = self.heads * QB
        return pl.pallas_call(
            functools.partial(attend_kernel, self.heads),
            grid_spec=pltpu.PrefetchScalarGridSpec(
                num_scalar_prefetch=3,
                grid=(self.steps,),
                in_specs=[query, key, keyt, info],
                out_specs=[query, lse],
                scratch_shapes=[pltpu.VMEM((LEN // KB, KB, lanes), F32)],
            ),
            out_shape=[
                jax.ShapeDtypeStruct(q.shape, BF),
                jax.ShapeDtypeStruct((self.steps, 8, lanes), F32),
            ],
            cost_estimate=self._cost(2),
            name="attend",
        )(self.place, self.low, self.top, q, keys, values_t, self.info)

    def backward(self, q, o, do, keys, values, keys_t, lse_in):
        query, key, keyt, info, lse = self._specs()
        per_seq = self.per_seq
        return pl.pallas_call(
            functools.partial(attend_back_kernel, self.heads, per_seq),
            grid_spec=pltpu.PrefetchScalarGridSpec(
                num_scalar_prefetch=3,
                grid=(self.steps,),
                in_specs=[query, query, query, key, key, keyt, info, lse],
                out_specs=[query, pl.BlockSpec((1, LEN, 2 * HD), lambda i, *_: (i // per_seq, 0, 0))],
                scratch_shapes=[pltpu.VMEM((LEN, HD), F32), pltpu.VMEM((LEN, HD), F32)],
            ),
            out_shape=[
                jax.ShapeDtypeStruct(q.shape, BF),
                jax.ShapeDtypeStruct((self.seqs, LEN, 2 * HD), BF),
            ],
            cost_estimate=self._cost(5),
            name="attend_back",
        )(self.place, self.low, self.top, q, o, do, keys, values, keys_t, self.info, lse_in)


def key_chunks(keys):
    seqs = keys.shape[0]
    return keys.reshape(seqs, LEN // KB, KB, HD).transpose(0, 1, 3, 2)


def _hop(v, axis, mask):
    size = lax.axis_size(axis)
    return lax.ppermute(v, axis, [(i, i ^ mask) for i in range(size)])


def _half(rows):
    return rows // 2 // 16 * 16


class Square:
    def __init__(self, blocks):
        self.count = blocks
        me = lax.axis_index("tensor")
        self.place = me ^ jnp.arange(blocks, dtype=jnp.int32)

    def gather(self, v):
        h = _half(v.shape[0])
        bx, by = _hop(v, "tensor", 1), _hop(v, "tensor", 2)
        top, bottom = _hop(by[:h], "tensor", 1), _hop(bx[h:], "tensor", 2)
        return [v, bx, by, jnp.concatenate([top, bottom], axis=0)]

    def scatter(self, make):
        corner = make(3).astype(BF)
        h = _half(corner.shape[0])
        to_y, to_x = _hop(corner[:h], "tensor", 1), _hop(corner[h:], "tensor", 2)
        zero = [(0, 0)] * (corner.ndim - 1)
        py = make(2) + jnp.pad(to_y.astype(F32), [(0, corner.shape[0] - h)] + zero)
        px = make(1) + jnp.pad(to_x.astype(F32), [(h, 0)] + zero)
        ry, rx = _hop(py.astype(BF), "tensor", 2), _hop(px.astype(BF), "tensor", 1)
        return make(0) + rx.astype(F32) + ry.astype(F32)

    def ordered(self, stacked):
        return jnp.take(stacked, self.place, axis=0, mode="clip")

    def relative(self, stacked):
        return jnp.take(stacked, self.place, axis=0, mode="clip")


class Plain:
    def __init__(self, blocks):
        self.count = blocks
        self.place = jnp.arange(blocks, dtype=jnp.int32)

    def gather(self, v):
        whole = lax.all_gather(v, "tensor", axis=0)
        return [whole[i] for i in range(self.count)]

    def scatter(self, make):
        whole = jnp.concatenate([make(i).astype(BF) for i in range(self.count)], axis=0)
        return lax.psum_scatter(whole, "tensor", scatter_dimension=0, tiled=True).astype(F32)

    def ordered(self, stacked):
        return stacked

    def relative(self, stacked):
        return stacked


def after(value, *others):
    return lax.optimization_barrier((value, others))[0]


def total_over(v, *axes):
    for axis in axes:
        mask = 1
        while mask < lax.axis_size(axis):
            v = v + _hop(v, axis, mask)
            mask *= 2
    return v


def norm_parts(v):
    average = jnp.mean(v, axis=-1, keepdims=True)
    centered = v - average
    rate = lax.rsqrt(jnp.mean(centered * centered, axis=-1, keepdims=True) + 1e-05)
    return centered * rate, rate


def norm_back(grad, hat, rate, gain):
    scaled = grad * gain
    return rate * (
        scaled
        - jnp.mean(scaled, axis=-1, keepdims=True)
        - hat * jnp.mean(scaled * hat, axis=-1, keepdims=True)
    )


GELU_A = math.sqrt(2.0 / math.pi)
GELU_B = 0.044715


def gelu_both(a):
    square = a * a
    t = jnp.tanh(GELU_A * (a + GELU_B * square * a))
    half = 0.5 * (1.0 + t)
    slope = half + 0.5 * a * (1.0 - t * t) * (GELU_A * (1.0 + 3.0 * GELU_B * square))
    return a * half, slope


def dot(a, b):
    return jnp.dot(a, b, preferred_element_type=F32)


def dot_t(a, b):
    return lax.dot_general(a, b, (((1,), (1,)), ((), ())), preferred_element_type=F32)


def dot_tokens(a, b):
    return lax.dot_general(a, b, (((0,), (0,)), ((), ())), preferred_element_type=F32)


def per_device(
    tokens,
    segment,
    cotangent,
    ln1_gain,
    ln1_shift,
    w_query,
    b_query,
    w_keyval,
    b_value,
    w_out,
    b_out,
    ln2_gain,
    ln2_shift,
    w_in,
    b_in,
    w_back,
    b_back,
):
    dp, nt = lax.axis_size("dp"), lax.axis_size("tensor")
    me_dp, me_t = lax.axis_index("dp"), lax.axis_index("tensor")
    rows, width = tokens.shape
    heads = b_query.shape[0] // HD
    wide = heads * HD
    inputs = tokens.astype(F32)
    net = Square(nt) if nt == 4 else Plain(nt)

    kv_rows = w_keyval.size // wide
    out_rows = w_out.size // wide
    pack = jnp.concatenate(
        [
            w_query.astype(BF),
            w_keyval.astype(BF).reshape(kv_rows, wide),
            w_out.astype(BF).reshape(out_rows, wide),
        ],
        axis=0,
    )
    packed = lax.all_gather(pack, "dp", axis=0)
    query_full = packed[:, : w_query.shape[0]].reshape(width, wide)
    keyval_own = packed[:, w_query.shape[0] : w_query.shape[0] + kv_rows]
    output_full = (
        packed[:, w_query.shape[0] + kv_rows :]
        .reshape(dp, wide, w_out.shape[1])
        .transpose(1, 0, 2)
        .reshape(wide, width)
    )
    inner_full = lax.all_gather(w_in.astype(BF), "dp", axis=0, tiled=True)
    down_full = lax.all_gather(w_back.astype(BF), "dp", axis=1, tiled=True)
    keyval_own = keyval_own.reshape(dp * w_keyval.shape[0], 2 * HD)
    keyval_all = net.ordered(jnp.stack(net.gather(keyval_own)))
    keyval_full = (
        keyval_all.reshape(nt, dp, w_keyval.shape[0], 2 * HD).transpose(1, 0, 2, 3).reshape(width, 2 * HD)
    )

    hat1, rate1 = norm_parts(inputs)
    normed1 = (hat1 * ln1_gain + ln1_shift).astype(BF)
    n1 = net.gather(normed1)
    cot = net.gather(after(cotangent, n1[-1]))
    queries = jnp.stack([(dot(n, query_full) + b_query).astype(BF) for n in n1])
    bias = jnp.concatenate([jnp.zeros_like(b_value), b_value])
    keyval = jnp.stack(net.gather((dot(normed1, keyval_full) + bias).astype(BF)))
    seqs = nt * rows // LEN
    keyval = net.ordered(keyval).reshape(seqs, LEN, 2 * HD)
    keys, values = keyval[..., :HD], keyval[..., HD:]
    attention = Attention(segment, net.place, rows, heads)
    mixture, lse = attention.forward(queries, keys, key_chunks(values))
    mixture = after(mixture, cot[-1])
    attended = net.scatter(lambda i: dot(mixture[i], output_full))
    hidden = inputs + attended + b_out

    hat2, rate2 = norm_parts(hidden)
    normed2 = (hat2 * ln2_gain + ln2_shift).astype(BF)
    n2 = net.gather(normed2)
    act, slope = [], []
    for n in n2:
        a, g = gelu_both(dot(n, inner_full) + b_in)
        act.append(a.astype(BF))
        slope.append(g.astype(BF))
    cot_all = jnp.concatenate(cot, axis=0)
    act_all = jnp.concatenate(act, axis=0)
    down_grad = dot_tokens(act_all, cot_all).astype(BF)
    down_total = lax.psum_scatter(down_grad, "dp", scatter_dimension=1, tiled=True).astype(F32)
    down_full = after(down_full, down_grad)
    pre_grad = [(dot_t(c, down_full) * g.astype(F32)).astype(BF) for c, g in zip(cot, slope)]
    second_grad = net.scatter(lambda i: dot_t(pre_grad[i], inner_full))
    pre_all = jnp.concatenate(pre_grad, axis=0)
    inner_grad = dot_tokens(jnp.concatenate(n2, axis=0), pre_all).astype(BF)
    inner_total = lax.psum_scatter(after(inner_grad, down_total), "dp", scatter_dimension=0, tiled=True).astype(F32)
    inner_bias = jnp.sum(pre_all, axis=0, dtype=F32)
    second_grad = after(second_grad, inner_grad)

    act = after(act, second_grad)
    feed = net.scatter(lambda i: dot(act[i], down_full))
    output = (hidden + feed + b_back).astype(BF)

    grad_out = cotangent.astype(F32)
    hidden_grad = grad_out + norm_back(second_grad, hat2, rate2, ln2_gain)
    hid = net.gather(hidden_grad.astype(BF))
    mixture_grad = jnp.stack([dot_t(h, output_full).astype(BF) for h in hid])
    query_low, keyval_part = attention.backward(
        queries, mixture, after(mixture_grad, down_total), keys, values, key_chunks(keys), lse
    )
    output_grad = dot_tokens(mixture.reshape(nt * rows, wide), jnp.concatenate(hid, axis=0)).astype(BF)
    output_total = lax.psum_scatter(after(output_grad, inner_total), "dp", scatter_dimension=1, tiled=True).astype(F32)
    query_grad = dot_tokens(jnp.concatenate(n1, axis=0), query_low.reshape(nt * rows, wide)).astype(BF)
    query_bias = jnp.sum(query_low, axis=(0, 1), dtype=F32)

    parts = net.relative(keyval_part.reshape(nt, rows, 2 * HD))
    keyval_low = net.scatter(lambda i: parts[i].astype(F32)).astype(BF)
    normed_grad = net.scatter(lambda i: dot_t(query_low[i], query_full)) + dot_t(keyval_low, keyval_full)
    keyval_grad = dot_tokens(normed1, keyval_low).reshape(dp, nt, w_keyval.shape[0], 2 * HD)
    keyval_grad = keyval_grad.transpose(1, 0, 2, 3).reshape(nt, dp * w_keyval.shape[0], 2 * HD)
    keyval_grad = net.relative(keyval_grad)
    keyval_grad = net.scatter(lambda i: keyval_grad[i]).astype(BF)
    query_pack = jnp.concatenate(
        [query_grad.reshape(dp, w_query.shape[0], wide), keyval_grad.reshape(dp, kv_rows, wide)], axis=1
    )
    query_total = lax.psum_scatter(after(query_pack, output_total), "dp", scatter_dimension=0, tiled=True)[0].astype(F32)
    keyval_total = query_total[w_query.shape[0] :].reshape(w_keyval.shape)
    query_total = query_total[: w_query.shape[0]]

    normed_grad = after(normed_grad, inner_total)
    tokens_grad = (hidden_grad + norm_back(normed_grad, hat1, rate1, ln1_gain)).astype(BF)

    early = jnp.concatenate(
        [
            jnp.sum(second_grad * hat2, axis=0),
            jnp.sum(second_grad, axis=0),
            jnp.sum(hidden_grad, axis=0),
            jnp.sum(grad_out, axis=0),
        ]
    )
    early = total_over(early.reshape(-1, 128), "tensor", "dp").reshape(4, width)
    local = total_over(jnp.concatenate([inner_bias, query_bias]).reshape(-1, 128), "dp").reshape(-1)
    late = jnp.concatenate(
        [
            jnp.sum(normed_grad * hat1, axis=0),
            jnp.sum(normed_grad, axis=0),
            jnp.sum(keyval_low[:, HD:], axis=0, dtype=F32),
        ]
    )
    late = total_over(late.reshape(-1, 128), "tensor", "dp").reshape(-1)
    me = me_dp * nt + me_t

    def own(v):
        part = v.shape[-1] // (dp * nt)
        return lax.dynamic_slice_in_dim(v, me * part, part, axis=v.ndim - 1)

    early = own(early)
    return (
        output,
        tokens_grad,
        own(late[:width]),
        own(late[width : 2 * width]),
        query_total,
        local[b_in.shape[0] :],
        keyval_total,
        own(late[2 * width :]),
        output_total,
        early[2],
        early[0],
        early[1],
        inner_total,
        local[: b_in.shape[0]],
        down_total,
        early[3],
    )


def solution(mesh):
    return jax.shard_map(
        per_device,
        mesh=mesh,
        in_specs=(
            P(("dp", "tensor"), None),
            P("dp"),
            P(("dp", "tensor"), None),
            P(),
            P(),
            P("dp", "tensor"),
            P("tensor"),
            P(("dp", "tensor"), None),
            P(),
            P("tensor", "dp"),
            P(),
            P(),
            P(),
            P("dp", "tensor"),
            P("tensor"),
            P("tensor", "dp"),
            P(),
        ),
        out_specs=(
            P(("dp", "tensor"), None),
            P(("dp", "tensor"), None),
            P(("dp", "tensor")),
            P(("dp", "tensor")),
            P("dp", "tensor"),
            P("tensor"),
            P(("dp", "tensor"), None),
            P(("dp", "tensor")),
            P("tensor", "dp"),
            P(("dp", "tensor")),
            P(("dp", "tensor")),
            P(("dp", "tensor")),
            P("dp", "tensor"),
            P("tensor"),
            P("tensor", "dp"),
            P(("dp", "tensor")),
        ),
        check_vma=False,
    )
```

time: 1410 us -> 789 us (0.56)
  waiting for transfers between devices: 955 us -> 327 us
  starting transfers between devices: 1.54 us -> 90.2 us
  matrix products: 260 us -> 175 us
  blocking collectives: 66.6 us -> 0 us
  local copies, waits for them, and re-layouts: 16.6 us -> 80.1 us
  Pallas kernels: 0 us -> 34.6 us
  other arithmetic: 84.4 us -> 55.4 us
    all_gather x9 -> x3, waiting for transfers between devices: 475 us -> 0.01 us  [the longest x1 0.01 us: per_device(): packed = lax.all_gather(pack, 'dp', axis=0)]
    reduce_scatter x10 -> x4, waiting for transfers between devices: 479 us -> 47.5 us  [the longest x1 47.5 us: per_device(): lax.psum_scatter(down_grad, 'dp', scatter_dimension=1, tiled=True)]
    ppermute x0 -> x61, waiting for transfers between devices: none -> 279 us  [_hop(): return lax.ppermute(v, axis, [(i, i ^ mask) for i in range(size)])]
    ppermute x0 -> x61, starting transfers between devices: none -> 89.8 us  [_hop(): return lax.ppermute(v, axis, [(i, i ^ mask) for i in range(size)])]
    dot_general x21 -> x39, matrix products: 260 us -> 175 us  [the longest x17 75.9 us: dot_t(): lax.dot_general(a, b, (((1,), (1,)), ((), ())), preferred_element_type=F32)]
    unnamed x1 -> x0, blocking collectives: 40.4 us -> none
    pallas_call x0 -> x2, Pallas kernels: none -> 34.6 us  [the longest x1 18.4 us: backward(): pl.pallas_call(functools.partial(attend_back_kernel, self.heads, per_seq)...]
    convert_element_type x14, other arithmetic: 50.7 us -> 19.4 us  [the longest x1 2.79 us: per_device(): lax.psum_scatter(after(inner_grad, down_total), 'dp', scatter_dimension=0...]
  transfers between devices with their start and end apart: 19 -> 68, of which waited for: 17 -> 43; matrix products, arithmetic and copies ran while one was open for 15% -> 37% of each run, Pallas kernels for 0% -> 4%
where the time goes in v1:
time: 789 us; the launch traced here: 778 us
  waiting for transfers between devices  327 us (41%)
  matrix products  175 us (22%)
  starting transfers between devices  90.2 us (11%)
  local copies, waits for them, and re-layouts  80.1 us (10%)
  other arithmetic  55.4 us (7%)
  Pallas kernels  34.6 us (4%)
  between operations  16 us (2%)
    ppermute x61, waiting for transfers between devices, _hop(): return lax.ppermute(v, axis, [(i, i ^ mask) for i in range(size)])  279 us
    ppermute x61, starting transfers between devices, _hop(): return lax.ppermute(v, axis, [(i, i ^ mask) for i in range(size)])  89.8 us
    dot_general x17, matrix products, dot_t(): lax.dot_general(a, b, (((1,), (1,)), ((), ())), preferred_element_type=F32)  75.9 us
    dot_general x17, matrix products, dot(): return jnp.dot(a, b, preferred_element_type=F32)  51.2 us
    dot_general x5, matrix products, dot_tokens(): lax.dot_general(a, b, (((0,), (0,)), ((), ())), preferred_element_type=F32)  47.8 us
    reduce_scatter x1, waiting for transfers between devices, per_device(): lax.psum_scatter(down_grad, 'dp', scatter_dimension=1, tiled=True)  47.5 us
    unnamed x183, local copies, waits for them, and re-layouts  29.2 us
    pallas_call x1, Pallas kernels, backward(): pl.pallas_call(functools.partial(attend_back_kernel, self.heads, per_seq)...  18.4 us
  transfers between devices with their start and end apart: 68, of which 43 were waited for; matrix products, arithmetic and copies ran while one was open for 37% of the time, Pallas kernels for 4%

profile of v1, /device:TPU:0, one launch (start us, length us, event | category | flops | bytes accessed | tf_op | source)
XLA Modules:
  0.0 778.1 jit_solution(17284501837064627580)
XLA Ops:
  17.7 3.0 collective-permute-start.1
  22.2 28.7 %collective-permute-done.1 = bf16[336,2048]{1,0:T(8,128)(2,1)S(1)} collective-permute-done((bf16[336,2048]{1,0:T(8,128)(2,1)S(1)}, bf16[336,2048]{1,0:T(8,128)(2,1)S(1)}, u32[]{:S(2)}, u32[]{:S(2)}) %collective-permute-start.1) | collective-permute-done | bytes 1376288 | tf_op jit(solution)/shard_map/ppermute | solution.py:191
  57.8 2.6 constant_dynamic-update-slice_fusion.17
  61.6 6.5 collective-permute-done.2
  70.3 2.9 collective-permute-done.3
  80.9 24.5 %collective-permute-done.12 = bf16[336,2048]{1,0:T(8,128)(2,1)} collective-permute-done((bf16[336,2048]{1,0:T(8,128)(2,1)S(1)}, bf16[336,2048]{1,0:T(8,128)(2,1)}, u32[]{:S(2)}, u32[]{:S(2)}) %collective-permute-start.12) | collective-permute-done | bytes 1376288 | tf_op jit(solution)/shard_map/ppermute | solution.py:191
  111.2 2.6 constant_dynamic-update-slice_fusion.7
  113.8 2.6 constant_dynamic-update-slice_fusion.6
  116.4 5.4 collective-permute-done.13
  130.6 2.7 fusion.123
  146.9 2.9 copy.44
  153.3 2.8 gather_fusion
  172.6 2.5 gather_fusion.1
  179.0 16.2 %attend.1 = (bf16[4,336,512]{2,1,0:T(8,128)(2,1)}, f32[12,8,448]{2,1,0:T(8,128)}) custom-call(s32[4]{0:T(128)} %iota_xor_fusion.place_ref, s32[12]{0:T(128)} %get-tuple-element.102.low_ref, s32[12]{0:T(128)} %get-tuple-element.103.top_ref, bf16[4,336,512]{2,1,0:T(8,128)(2,1)} %pad_maximum_fusion.2.q_ref, bf16[1,1344,128]{2,1,0:T(8,128)(2,1)} %get-tuple-element.83.k_ref, ...), custom_call_target="tpu_custom_call" | custom-call | flops 1849688064 | bytes 5505024 | tf_op jit(solution)/shard_map/attend/pallas_call | solution.py:146
  199.2 10.5 %collective-permute-done.18 = bf16[160,2048]{1,0:T(8,128)(2,1)S(1)} collective-permute-done((bf16[160,2048]{1,0:T(8,128)(2,1)S(1)}, bf16[160,2048]{1,0:T(8,128)(2,1)S(1)}, u32[]{:S(2)}, u32[]{:S(2)}) %collective-permute-start.18) | collective-permute-done | bytes 655392 | tf_op jit(solution)/shard_map/ppermute | solution.py:191
  212.6 2.8 collective-permute-done.16
  218.3 23.6 %collective-permute-done.19 = bf16[336,2048]{1,0:T(8,128)(2,1)S(1)} collective-permute-done((bf16[336,2048]{1,0:T(8,128)(2,1)S(1)}, bf16[336,2048]{1,0:T(8,128)(2,1)S(1)}, u32[]{:S(2)}, u32[]{:S(2)}) %collective-permute-start.19) | collective-permute-done | bytes 1376288 | tf_op jit(solution)/shard_map/ppermute | solution.py:191
  247.9 27.1 %collective-permute-done.20 = bf16[336,2048]{1,0:T(8,128)(2,1)S(1)} collective-permute-done((bf16[336,2048]{1,0:T(8,128)(2,1)S(1)}, bf16[336,2048]{1,0:T(8,128)(2,1)S(1)}, u32[]{:S(2)}, u32[]{:S(2)}) %collective-permute-start.20) | collective-permute-done | bytes 1376288 | tf_op jit(solution)/shard_map/ppermute | solution.py:191
  278.7 10.1 %collective-permute-done.22 = bf16[160,2048]{1,0:T(8,128)(2,1)} collective-permute-done((bf16[160,2048]{1,0:T(8,128)(2,1)S(1)}, bf16[160,2048]{1,0:T(8,128)(2,1)}, u32[]{:S(2)}, u32[]{:S(2)}) %collective-permute-start.22) | collective-permute-done | bytes 655392 | tf_op jit(solution)/shard_map/ppermute | solution.py:191
  290.5 8.8 %multiply_convert_fusion = (bf16[336,2048]{1,0:T(8,128)(2,1)S(1)}, f32[336,2048]{1,0:T(8,128)}) fusion(f32[2048]{0:T(1024)S(1)} %copy-done.67, bf16[2048,2048]{1,0:T(8,128)(2,1)} %all-gather.5.cloned.1.call-done, bf16[176,2048]{1,0:T(8,128)(2,1)S(1)} %collective-permute-done.23, bf16[160,2048]{1,0:T(8,128)(2,1)} %collective-permute-done.22), kind=kOutput, calls=%fused_computation.71 | convolution fusion | flops 2828206080 | bytes 13901824 | tf_op jit(solution)/shard_map/dot_general | solution.py:289
  299.3 5.1 multiply_convert_fusion.1
  304.4 5.5 multiply_convert_fusion.2
  310.0 5.1 multiply_convert_fusion.3
  316.2 17.7 %convolution_convert_fusion.1 = bf16[2048,2048]{1,0:T(8,128)(2,1)} fusion(bf16[1344,2048]{1,0:T(8,128)(2,1)} %get-tuple-element.78, bf16[336,2048]{1,0:T(8,128)(2,1)S(1)} %get-tuple-element.40, bf16[336,2048]{1,0:T(8,128)(2,1)S(1)} %get-tuple-element.41, bf16[336,2048]{1,0:T(8,128)(2,1)S(1)} %get-tuple-element.39, bf16[336,2048]{1,0:T(8,128)(2,1)S(1)} %get-tuple-element.38), kind=kOutput, calls=%fused_computation.7 | convolution fusion | flops 11300503552 | bytes 19398656 | tf_op jit(solution)/shard_map/dot_general | solution.py:297
  339.5 8.5 %fusion.31 = bf16[336,2048]{1,0:T(8,128)(2,1)S(1)} fusion(bf16[336,2048]{1,0:T(8,128)(2,1)S(1)} %copy-done.13, bf16[2048,2048]{1,0:T(8,128)(2,1)} %all-gather.7.cloned.1.call-done, f32[336,2048]{1,0:T(8,128)} %get-tuple-element.101), kind=kOutput, calls=%fused_computation.91 | convolution fusion | flops 2832334848 | bytes 13893632 | tf_op jit(solution)/shard_map/dot_general | solution.py:293
  348.1 6.2 fusion.33
  354.3 9.3 %fusion.32 = bf16[336,2048]{1,0:T(8,128)(2,1)S(1)} fusion(bf16[336,2048]{1,0:T(8,128)(2,1)} %collective-permute-done.14, bf16[2048,2048]{1,0:T(8,128)(2,1)} %all-gather.7.cloned.1.call-done, f32[336,2048]{1,0:T(8,128)} %get-tuple-element.99), kind=kOutput, calls=%fused_computation.92 | convolution fusion | flops 2832334848 | bytes 13893632 | tf_op jit(solution)/shard_map/dot_general | solution.py:293
  363.6 9.1 %fusion.34 = bf16[336,2048]{1,0:T(8,128)(2,1)S(1)} fusion(bf16[336,2048]{1,0:T(8,128)(2,1)} %collective-permute-done.12, bf16[2048,2048]{1,0:T(8,128)(2,1)} %all-gather.7.cloned.1.call-done, f32[336,2048]{1,0:T(8,128)S(1)} %copy-done.69), kind=kOutput, calls=%fused_computation.94 | convolution fusion | flops 2832334848 | bytes 13893632 | tf_op jit(solution)/shard_map/dot_general | solution.py:293
  373.8 15.9 %convolution_convert_fusion = bf16[2048,2048]{1,0:T(8,128)(2,1)} fusion(bf16[1344,2048]{1,0:T(8,128)(2,1)S(1)} %bitcast.266, bf16[336,2048]{1,0:T(8,128)(2,1)S(1)} %fusion.33, bf16[336,2048]{1,0:T(8,128)(2,1)S(1)} %fusion.34, bf16[336,2048]{1,0:T(8,128)(2,1)S(1)} %fusion.32, bf16[336,2048]{1,0:T(8,128)(2,1)S(1)} %fusion.31), kind=kOutput, calls=%fused_computation.6 | convolution fusion | flops 11300503552 | bytes 19398656 | tf_op jit(solution)/shard_map/dot_general | solution.py:297
  389.7 47.5 %reduce-scatter.5.cloned.1.call-done = bf16[2048,256]{1,0:T(8,128)(2,1)} async-done(((bf16[2048,2048]{1,0:T(8,128)(2,1)}), bf16[2048,256]{1,0:T(8,128)(2,1)}) %reduce-scatter.5.cloned.1.call-update) | async-done | bytes 1048592 | tf_op jit(solution)/shard_map/reduce_scatter | solution.py:381
  437.2 2.7 convert_element_type.352
  440.0 6.5 convolution_convert_fusion.5
  449.7 11.5 %collective-permute-done.26 = bf16[160,2048]{1,0:T(8,128)(2,1)S(1)} collective-permute-done((bf16[160,2048]{1,0:T(8,128)(2,1)S(1)}, bf16[160,2048]{1,0:T(8,128)(2,1)S(1)}, u32[]{:S(2)}, u32[]{:S(2)}) %collective-permute-start.26) | collective-permute-done | bytes 655392 | tf_op jit(solution)/shard_map/ppermute | solution.py:191
  461.2 6.5 add_convert_fusion.5
  469.3 4.3 add_convert_fusion.7
  475.2 3.1 fusion.125
  478.3 18.8 %collective-permute-done.27 = bf16[336,2048]{1,0:T(8,128)(2,1)S(1)} collective-permute-done((bf16[336,2048]{1,0:T(8,128)(2,1)S(1)}, bf16[336,2048]{1,0:T(8,128)(2,1)S(1)}, u32[]{:S(2)}, u32[]{:S(2)}) %collective-permute-start.27) | collective-permute-done | bytes 1376288 | tf_op jit(solution)/shard_map/ppermute | solution.py:191
  497.1 5.8 collective-permute-done.25
  503.7 3.1 convolution_convert_fusion.4
  509.0 10.6 %collective-permute-done.30 = bf16[160,2048]{1,0:T(8,128)(2,1)S(1)} collective-permute-done((bf16[160,2048]{1,0:T(8,128)(2,1)S(1)}, bf16[160,2048]{1,0:T(8,128)(2,1)S(1)}, u32[]{:S(2)}, u32[]{:S(2)}) %collective-permute-start.30) | collective-permute-done | bytes 655392 | tf_op jit(solution)/shard_map/ppermute | solution.py:191
  519.7 3.1 add_convert_fusion.3
  524.0 3.1 add_convert_fusion.4
  529.3 3.3 fusion.126
  532.6 19.3 %collective-permute-done.31 = bf16[336,2048]{1,0:T(8,128)(2,1)S(1)} collective-permute-done((bf16[336,2048]{1,0:T(8,128)(2,1)S(1)}, bf16[336,2048]{1,0:T(8,128)(2,1)S(1)}, u32[]{:S(2)}, u32[]{:S(2)}) %collective-permute-start.31) | collective-permute-done | bytes 1376288 | tf_op jit(solution)/shard_map/ppermute | solution.py:191
  553.9 3.4 fusion.119
  563.6 2.9 fusion.49
  566.5 19.9 %collective-permute-done.56 = f32[64,128]{1,0:T(8,128)S(1)} collective-permute-done((f32[64,128]{1,0:T(8,128)S(1)}, f32[64,128]{1,0:T(8,128)S(1)}, u32[]{:S(2)}, u32[]{:S(2)}) %collective-permute-start.56) | collective-permute-done | bytes 32800 | tf_op jit(solution)/shard_map/ppermute | solution.py:191
  592.4 2.5 fusion.50
  605.8 4.7 convolution_convert_fusion.2
  610.5 18.4 %attend_back.1 = (bf16[4,336,512]{2,1,0:T(8,128)(2,1)}, bf16[1,1344,256]{2,1,0:T(8,128)(2,1)}) custom-call(s32[4]{0:T(128)} %iota_xor_fusion.place_ref, s32[12]{0:T(128)} %get-tuple-element.102.low_ref, s32[12]{0:T(128)} %get-tuple-element.103.top_ref, bf16[4,336,512]{2,1,0:T(8,128)(2,1)} %pad_maximum_fusion.2.q_ref, ...), custom_call_target="tpu_custom_call" | custom-call | flops 4624220160 | bytes 5505024 | tf_op jit(solution)/shard_map/attend_back/pallas_call | solution.py:166
  632.9 2.8 convert_element_type.369
  638.3 17.6 %collective-permute-start.59 = (f32[64,128]{1,0:T(8,128)S(1)}, f32[64,128]{1,0:T(8,128)}, u32[]{:S(2)}, u32[]{:S(2)}) collective-permute-start(f32[64,128]{1,0:T(8,128)S(1)} %add.424), channel_id=1, source_target_pairs={{0,8},{4,12},{8,0},{12,4},{16,24},{20,28},{24,16},{28,20},{1,9},{5... | collective-permute-start | bytes 98312 | tf_op jit(solution)/shard_map/ppermute | solution.py:191
  661.7 3.9 convert_reduce_fusion
  672.2 3.8 gather_fusion.3
  687.0 7.4 convolution_convert_fusion.3
  694.4 9.4 %collective-permute-done.50 = bf16[512,256]{1,0:T(8,128)(2,1)S(1)} collective-permute-done((bf16[512,256]{1,0:T(8,128)(2,1)S(1)}, bf16[512,256]{1,0:T(8,128)(2,1)S(1)}, u32[]{:S(2)}, u32[]{:S(2)}) %collective-permute-start.50) | collective-permute-done | bytes 262176 | tf_op jit(solution)/shard_map/ppermute | solution.py:191
  704.5 4.0 add_convert_fusion
  711.2 3.8 add_convert_fusion.1
  724.5 2.9 collective-permute-start.55
  727.4 2.6 fusion.80
  730.2 7.6 collective-permute-done.39
  737.8 6.1 collective-permute-done.37
  743.9 2.5 add_add_fusion
  756.6 2.7 collective-permute-start.47
  (441 shorter events, 212.7 us)
Async XLA Ops:
  7.2 119.1 %all-gather.9.cloned.1.call-start = ((), (), s32[]{:S(2)}) async-start(), calls=%async_computation.10 | async-start | bytes 5013504 | tf_op jit(solution)/shard_map/all_gather | solution.py:337
  13.9 276.6 %all-gather.5.cloned.1.call-start = ((), (), s32[]{:S(2)}) async-start(), calls=%async_computation.4 | async-start | bytes 9437184 | tf_op jit(solution)/shard_map/all_gather | solution.py:346
  15.1 324.4 %all-gather.7.cloned.1.call-start = ((), (), s32[]{:S(2)}) async-start(), calls=%async_computation.5 | async-start | bytes 9437184 | tf_op jit(solution)/shard_map/all_gather | solution.py:347
  17.7 33.2 %collective-permute-start.1 = (bf16[336,2048]{1,0:T(8,128)(2,1)S(1)}, bf16[336,2048]{1,0:T(8,128)(2,1)S(1)}, u32[]{:S(2)}, u32[]{:S(2)}) collective-permute-start(bf16[336,2048]{1,0:T(8,128)(2,1)S(1)} %get-tuple-element.63), channel_id=1, source_target_pairs={{0,2},{1,3},{2,0},{3,1},{4,6},{5,7},{6,4},{7,5},{8,10},{9,11},{10,... | collective-permute-start | bytes 4128776 | tf_op jit(solution)/shard_map/ppermute | solution.py:191
  20.7 34.3 %collective-permute-start = (bf16[336,2048]{1,0:T(8,128)(2,1)S(1)}, bf16[336,2048]{1,0:T(8,128)(2,1)}, u32[]{:S(2)}, u32[]{:S(2)}) collective-permute-start(bf16[336,2048]{1,0:T(8,128)(2,1)S(1)} %get-tuple-element.63), channel_id=1, source_target_pairs={{0,1},{1,0},{2,3},{3,2},{4,5},{5,4},{6,7},{7,6},{8,9},{9,8},{10,11... | collective-permute-start | bytes 4128776 | tf_op jit(solution)/shard_map/ppermute | solution.py:191
  52.0 16.2 %collective-permute-start.2 = (bf16[160,2048]{1,0:T(8,128)(2,1)S(1)}, bf16[160,2048]{1,0:T(8,128)(2,1)}, u32[]{:S(2)}, u32[]{:S(2)}) collective-permute-start(bf16[160,2048]{1,0:T(8,128)(2,1)S(1)} %slice.285), channel_id=1, source_target_pairs={{0,1},{1,0},{2,3},{3,2},{4,5},{5,4},{6,7},{7,6},{8,9},{9,8},{10,11... | collective-permute-start | bytes 1966088 | tf_op jit(solution)/shard_map/ppermute | solution.py:191
  54.9 382.3 %reduce-scatter.5.cloned.1.call-start = ((), (), s32[]{:S(2)}) async-start(), calls=%async_computation.6 | async-start | bytes 9437184 | tf_op jit(solution)/shard_map/reduce_scatter | solution.py:381
  56.2 16.9 %collective-permute-start.3 = (bf16[176,2048]{1,0:T(8,128)(2,1)S(1)}, bf16[176,2048]{1,0:T(8,128)(2,1)S(1)}, u32[]{:S(2)}, u32[]{:S(2)}) collective-permute-start(bf16[176,2048]{1,0:T(8,128)(2,1)S(1)} %slice.286), channel_id=1, source_target_pairs={{0,2},{1,3},{2,0},{3,1},{4,6},{5,7},{6,4},{7,5},{8,10},{9,11},{10,... | collective-permute-start | bytes 2162696 | tf_op jit(solution)/shard_map/ppermute | solution.py:191
  75.3 30.1 %collective-permute-start.12 = (bf16[336,2048]{1,0:T(8,128)(2,1)S(1)}, bf16[336,2048]{1,0:T(8,128)(2,1)}, u32[]{:S(2)}, u32[]{:S(2)}) collective-permute-start(bf16[336,2048]{1,0:T(8,128)(2,1)S(1)} %copy-done.12), channel_id=1, source_target_pairs={{0,2},{1,3},{2,0},{3,1},{4,6},{5,7},{6,4},{7,5},{8,10},{9,11},{10,... | collective-permute-start | bytes 4128776 | tf_op jit(solution)/shard_map/ppermute | solution.py:191
  77.9 31.4 %collective-permute-start.14 = (bf16[336,2048]{1,0:T(8,128)(2,1)S(1)}, bf16[336,2048]{1,0:T(8,128)(2,1)}, u32[]{:S(2)}, u32[]{:S(2)}) collective-permute-start(bf16[336,2048]{1,0:T(8,128)(2,1)S(1)} %copy-done.12), channel_id=1, source_target_pairs={{0,1},{1,0},{2,3},{3,2},{4,5},{5,4},{6,7},{7,6},{8,9},{9,8},{10,11... | collective-permute-start | bytes 4128776 | tf_op jit(solution)/shard_map/ppermute | solution.py:191
  106.5 15.2 %collective-permute-start.13 = (bf16[160,2048]{1,0:T(8,128)(2,1)S(1)}, bf16[160,2048]{1,0:T(8,128)(2,1)S(1)}, u32[]{:S(2)}, u32[]{:S(2)}) collective-permute-start(bf16[160,2048]{1,0:T(8,128)(2,1)S(1)} %slice.294), channel_id=1, source_target_pairs={{0,1},{1,0},{2,3},{3,2},{4,5},{5,4},{6,7},{7,6},{8,9},{9,8},{10,11... | collective-permute-start | bytes 1966088 | tf_op jit(solution)/shard_map/ppermute | solution.py:191
  110.5 14.6 %collective-permute-start.15 = (bf16[176,2048]{1,0:T(8,128)(2,1)S(1)}, bf16[176,2048]{1,0:T(8,128)(2,1)S(1)}, u32[]{:S(2)}, u32[]{:S(2)}) collective-permute-start(bf16[176,2048]{1,0:T(8,128)(2,1)S(1)} %slice.295), channel_id=1, source_target_pairs={{0,2},{1,3},{2,0},{3,1},{4,6},{5,7},{6,4},{7,5},{8,10},{9,11},{10,... | collective-permute-start | bytes 2162696 | tf_op jit(solution)/shard_map/ppermute | solution.py:191
  128.1 9.0 %collective-permute-start.5 = (bf16[512,256]{1,0:T(8,128)(2,1)}, bf16[512,256]{1,0:T(8,128)(2,1)S(1)}, u32[]{:S(2)}, u32[]{:S(2)}) collective-permute-start(bf16[512,256]{1,0:T(8,128)(2,1)} %reshape.285), channel_id=1, source_target_pairs={{0,2},{1,3},{2,0},{3,1},{4,6},{5,7},{6,4},{7,5},{8,10},{9,11},{10,... | collective-permute-start | bytes 786440 | tf_op jit(solution)/shard_map/ppermute | solution.py:191
  129.1 9.9 %collective-permute-start.4 = (bf16[512,256]{1,0:T(8,128)(2,1)}, bf16[512,256]{1,0:T(8,128)(2,1)S(1)}, u32[]{:S(2)}, u32[]{:S(2)}) collective-permute-start(bf16[512,256]{1,0:T(8,128)(2,1)} %reshape.285), channel_id=1, source_target_pairs={{0,1},{1,0},{2,3},{3,2},{4,5},{5,4},{6,7},{7,6},{8,9},{9,8},{10,11... | collective-permute-start | bytes 786440 | tf_op jit(solution)/shard_map/ppermute | solution.py:191
  138.5 11.3 %collective-permute-start.6 = (bf16[256,256]{1,0:T(8,128)(2,1)}, bf16[256,256]{1,0:T(8,128)(2,1)}, u32[]{:S(2)}, u32[]{:S(2)}) collective-permute-start(bf16[256,256]{1,0:T(8,128)(2,1)} %slice.288), channel_id=1, source_target_pairs={{0,1},{1,0},{2,3},{3,2},{4,5},{5,4},{6,7},{7,6},{8,9},{9,8},{10,11... | collective-permute-start | bytes 393224 | tf_op jit(solution)/shard_map/ppermute | solution.py:191
  140.4 9.4 %collective-permute-start.7 = (bf16[256,256]{1,0:T(8,128)(2,1)}, bf16[256,256]{1,0:T(8,128)(2,1)}, u32[]{:S(2)}, u32[]{:S(2)}) collective-permute-start(bf16[256,256]{1,0:T(8,128)(2,1)} %slice.289), channel_id=1, source_target_pairs={{0,2},{1,3},{2,0},{3,1},{4,6},{5,7},{6,4},{7,5},{8,10},{9,11},{10,... | collective-permute-start | bytes 393224 | tf_op jit(solution)/shard_map/ppermute | solution.py:191
  160.1 5.5 collective-permute-start.8
  161.1 6.0 collective-permute-start.9
  165.6 6.0 collective-permute-start.11
  167.1 4.5 collective-permute-start.10
  197.2 12.5 %collective-permute-start.18 = (bf16[160,2048]{1,0:T(8,128)(2,1)S(1)}, bf16[160,2048]{1,0:T(8,128)(2,1)S(1)}, u32[]{:S(2)}, u32[]{:S(2)}) collective-permute-start(bf16[160,2048]{1,0:T(8,128)(2,1)S(1)} %slice.298), channel_id=1, source_target_pairs={{0,1},{1,0},{2,3},{3,2},{4,5},{5,4},{6,7},{7,6},{8,9},{9,8},{10,11... | collective-permute-start | bytes 1966088 | tf_op jit(solution)/shard_map/ppermute | solution.py:191
  198.5 16.9 %collective-permute-start.16 = (bf16[176,2048]{1,0:T(8,128)(2,1)S(1)}, bf16[176,2048]{1,0:T(8,128)(2,1)S(1)}, u32[]{:S(2)}, u32[]{:S(2)}) collective-permute-start(bf16[176,2048]{1,0:T(8,128)(2,1)S(1)} %slice.297), channel_id=1, source_target_pairs={{0,2},{1,3},{2,0},{3,1},{4,6},{5,7},{6,4},{7,5},{8,10},{9,11},{10,... | collective-permute-start | bytes 2162696 | tf_op jit(solution)/shard_map/ppermute | solution.py:191
  210.6 31.2 %collective-permute-start.19 = (bf16[336,2048]{1,0:T(8,128)(2,1)S(1)}, bf16[336,2048]{1,0:T(8,128)(2,1)S(1)}, u32[]{:S(2)}, u32[]{:S(2)}) collective-permute-start(bf16[336,2048]{1,0:T(8,128)(2,1)S(1)} %add_convert_fusion.12), channel_id=1, source_target_pairs={{0,2},{1,3},{2,0},{3,1},{4,6},{5,7},{6,4},{7,5},{8,10},{9,11},{10,... | collective-permute-start | bytes 4128776 | tf_op jit(solution)/shard_map/ppermute | solution.py:191
  216.3 25.6 %collective-permute-start.17 = (bf16[336,2048]{1,0:T(8,128)(2,1)S(1)}, bf16[336,2048]{1,0:T(8,128)(2,1)S(1)}, u32[]{:S(2)}, u32[]{:S(2)}) collective-permute-start(bf16[336,2048]{1,0:T(8,128)(2,1)S(1)} %add_convert_fusion.13), channel_id=1, source_target_pairs={{0,1},{1,0},{2,3},{3,2},{4,5},{5,4},{6,7},{7,6},{8,9},{9,8},{10,11... | collective-permute-start | bytes 4128776 | tf_op jit(solution)/shard_map/ppermute | solution.py:191
  245.4 29.7 %collective-permute-start.20 = (bf16[336,2048]{1,0:T(8,128)(2,1)S(1)}, bf16[336,2048]{1,0:T(8,128)(2,1)S(1)}, u32[]{:S(2)}, u32[]{:S(2)}) collective-permute-start(bf16[336,2048]{1,0:T(8,128)(2,1)S(1)} %get-tuple-element.65), channel_id=1, source_target_pairs={{0,1},{1,0},{2,3},{3,2},{4,5},{5,4},{6,7},{7,6},{8,9},{9,8},{10,11... | collective-permute-start | bytes 4128776 | tf_op jit(solution)/shard_map/ppermute | solution.py:191
  246.2 30.3 %collective-permute-start.21 = (bf16[336,2048]{1,0:T(8,128)(2,1)S(1)}, bf16[336,2048]{1,0:T(8,128)(2,1)S(1)}, u32[]{:S(2)}, u32[]{:S(2)}) collective-permute-start(bf16[336,2048]{1,0:T(8,128)(2,1)S(1)} %get-tuple-element.65), channel_id=1, source_target_pairs={{0,2},{1,3},{2,0},{3,1},{4,6},{5,7},{6,4},{7,5},{8,10},{9,11},{10,... | collective-permute-start | bytes 4128776 | tf_op jit(solution)/shard_map/ppermute | solution.py:191
  275.1 15.4 %collective-permute-start.23 = (bf16[176,2048]{1,0:T(8,128)(2,1)S(1)}, bf16[176,2048]{1,0:T(8,128)(2,1)S(1)}, u32[]{:S(2)}, u32[]{:S(2)}) collective-permute-start(bf16[176,2048]{1,0:T(8,128)(2,1)S(1)} %slice.300), channel_id=1, source_target_pairs={{0,2},{1,3},{2,0},{3,1},{4,6},{5,7},{6,4},{7,5},{8,10},{9,11},{10,... | collective-permute-start | bytes 2162696 | tf_op jit(solution)/shard_map/ppermute | solution.py:191
  276.5 12.2 %collective-permute-start.22 = (bf16[160,2048]{1,0:T(8,128)(2,1)S(1)}, bf16[160,2048]{1,0:T(8,128)(2,1)}, u32[]{:S(2)}, u32[]{:S(2)}) collective-permute-start(bf16[160,2048]{1,0:T(8,128)(2,1)S(1)} %slice.299), channel_id=1, source_target_pairs={{0,1},{1,0},{2,3},{3,2},{4,5},{5,4},{6,7},{7,6},{8,9},{9,8},{10,11... | collective-permute-start | bytes 1966088 | tf_op jit(solution)/shard_map/ppermute | solution.py:191
  333.9 299.0 %reduce-scatter.7.cloned.1.call-start = ((), (), s32[]{:S(2)}) async-start(), calls=%async_computation.7 | async-start | bytes 9437184 | tf_op jit(solution)/shard_map/reduce_scatter | solution.py:387
  439.9 276.1 %reduce-scatter.9.cloned.1.call-start = ((), (), s32[]{:S(2)}) async-start(), calls=%async_computation.8 | async-start | bytes 2359296 | tf_op jit(solution)/shard_map/reduce_scatter | solution.py:403
  446.6 14.7 %collective-permute-start.26 = (bf16[160,2048]{1,0:T(8,128)(2,1)S(1)}, bf16[160,2048]{1,0:T(8,128)(2,1)S(1)}, u32[]{:S(2)}, u32[]{:S(2)}) collective-permute-start(bf16[160,2048]{1,0:T(8,128)(2,1)S(1)} %slice.302), channel_id=1, source_target_pairs={{0,1},{1,0},{2,3},{3,2},{4,5},{5,4},{6,7},{7,6},{8,9},{9,8},{10,11... | collective-permute-start | bytes 1966088 | tf_op jit(solution)/shard_map/ppermute | solution.py:191
  448.2 21.1 %collective-permute-start.24 = (bf16[176,2048]{1,0:T(8,128)(2,1)S(1)}, bf16[176,2048]{1,0:T(8,128)(2,1)S(1)}, u32[]{:S(2)}, u32[]{:S(2)}) collective-permute-start(bf16[176,2048]{1,0:T(8,128)(2,1)S(1)} %slice.301), channel_id=1, source_target_pairs={{0,2},{1,3},{2,0},{3,1},{4,6},{5,7},{6,4},{7,5},{8,10},{9,11},{10,... | collective-permute-start | bytes 2162696 | tf_op jit(solution)/shard_map/ppermute | solution.py:191
  467.7 29.4 %collective-permute-start.27 = (bf16[336,2048]{1,0:T(8,128)(2,1)S(1)}, bf16[336,2048]{1,0:T(8,128)(2,1)S(1)}, u32[]{:S(2)}, u32[]{:S(2)}) collective-permute-start(bf16[336,2048]{1,0:T(8,128)(2,1)S(1)} %add_convert_fusion.5), channel_id=1, source_target_pairs={{0,2},{1,3},{2,0},{3,1},{4,6},{5,7},{6,4},{7,5},{8,10},{9,11},{10,... | collective-permute-start | bytes 4128776 | tf_op jit(solution)/shard_map/ppermute | solution.py:191
  473.6 29.3 %collective-permute-start.25 = (bf16[336,2048]{1,0:T(8,128)(2,1)}, bf16[336,2048]{1,0:T(8,128)(2,1)S(1)}, u32[]{:S(2)}, u32[]{:S(2)}) collective-permute-start(bf16[336,2048]{1,0:T(8,128)(2,1)} %add_convert_fusion.7), channel_id=1, source_target_pairs={{0,1},{1,0},{2,3},{3,2},{4,5},{5,4},{6,7},{7,6},{8,9},{9,8},{10,11... | collective-permute-start | bytes 4128776 | tf_op jit(solution)/shard_map/ppermute | solution.py:191
  506.8 12.9 %collective-permute-start.30 = (bf16[160,2048]{1,0:T(8,128)(2,1)S(1)}, bf16[160,2048]{1,0:T(8,128)(2,1)S(1)}, u32[]{:S(2)}, u32[]{:S(2)}) collective-permute-start(bf16[160,2048]{1,0:T(8,128)(2,1)S(1)} %slice.304), channel_id=1, source_target_pairs={{0,1},{1,0},{2,3},{3,2},{4,5},{5,4},{6,7},{7,6},{8,9},{9,8},{10,11... | collective-permute-start | bytes 1966088 | tf_op jit(solution)/shard_map/ppermute | solution.py:191
  508.4 15.5 %collective-permute-start.28 = (bf16[176,2048]{1,0:T(8,128)(2,1)S(1)}, bf16[176,2048]{1,0:T(8,128)(2,1)S(1)}, u32[]{:S(2)}, u32[]{:S(2)}) collective-permute-start(bf16[176,2048]{1,0:T(8,128)(2,1)S(1)} %slice.303), channel_id=1, source_target_pairs={{0,2},{1,3},{2,0},{3,1},{4,6},{5,7},{6,4},{7,5},{8,10},{9,11},{10,... | collective-permute-start | bytes 2162696 | tf_op jit(solution)/shard_map/ppermute | solution.py:191
  522.8 29.1 %collective-permute-start.31 = (bf16[336,2048]{1,0:T(8,128)(2,1)S(1)}, bf16[336,2048]{1,0:T(8,128)(2,1)S(1)}, u32[]{:S(2)}, u32[]{:S(2)}) collective-permute-start(bf16[336,2048]{1,0:T(8,128)(2,1)S(1)} %add_convert_fusion.3), channel_id=1, source_target_pairs={{0,2},{1,3},{2,0},{3,1},{4,6},{5,7},{6,4},{7,5},{8,10},{9,11},{10,... | collective-permute-start | bytes 4128776 | tf_op jit(solution)/shard_map/ppermute | solution.py:191
  527.1 26.8 %collective-permute-start.29 = (bf16[336,2048]{1,0:T(8,128)(2,1)S(1)}, bf16[336,2048]{1,0:T(8,128)(2,1)S(1)}, u32[]{:S(2)}, u32[]{:S(2)}) collective-permute-start(bf16[336,2048]{1,0:T(8,128)(2,1)S(1)} %add_convert_fusion.4), channel_id=1, source_target_pairs={{0,1},{1,0},{2,3},{3,2},{4,5},{5,4},{6,7},{7,6},{8,9},{9,8},{10,11... | collective-permute-start | bytes 4128776 | tf_op jit(solution)/shard_map/ppermute | solution.py:191
  559.2 28.7 %collective-permute-start.32 = (bf16[336,2048]{1,0:T(8,128)(2,1)}, bf16[336,2048]{1,0:T(8,128)(2,1)}, u32[]{:S(2)}, u32[]{:S(2)}) collective-permute-start(bf16[336,2048]{1,0:T(8,128)(2,1)} %get-tuple-element.61), channel_id=1, source_target_pairs={{0,1},{1,0},{2,3},{3,2},{4,5},{5,4},{6,7},{7,6},{8,9},{9,8},{10,11... | collective-permute-start | bytes 4128776 | tf_op jit(solution)/shard_map/ppermute | solution.py:191
  560.7 29.3 %collective-permute-start.33 = (bf16[336,2048]{1,0:T(8,128)(2,1)}, bf16[336,2048]{1,0:T(8,128)(2,1)}, u32[]{:S(2)}, u32[]{:S(2)}) collective-permute-start(bf16[336,2048]{1,0:T(8,128)(2,1)} %get-tuple-element.61), channel_id=1, source_target_pairs={{0,2},{1,3},{2,0},{3,1},{4,6},{5,7},{6,4},{7,5},{8,10},{9,11},{10,... | collective-permute-start | bytes 4128776 | tf_op jit(solution)/shard_map/ppermute | solution.py:191
  563.1 23.3 %collective-permute-start.56 = (f32[64,128]{1,0:T(8,128)S(1)}, f32[64,128]{1,0:T(8,128)S(1)}, u32[]{:S(2)}, u32[]{:S(2)}) collective-permute-start(f32[64,128]{1,0:T(8,128)S(1)} %pad_maximum_fusion.8), channel_id=1, source_target_pairs={{0,1},{1,0},{2,3},{3,2},{4,5},{5,4},{6,7},{7,6},{8,9},{9,8},{10,11... | collective-permute-start | bytes 98312 | tf_op jit(solution)/shard_map/ppermute | solution.py:191
  586.4 49.9 %collective-permute-start.57 = (f32[64,128]{1,0:T(8,128)S(1)}, f32[64,128]{1,0:T(8,128)}, u32[]{:S(2)}, u32[]{:S(2)}) collective-permute-start(f32[64,128]{1,0:T(8,128)S(1)} %fusion.118), channel_id=1, source_target_pairs={{0,2},{1,3},{2,0},{3,1},{4,6},{5,7},{6,4},{7,5},{8,10},{9,11},{10,... | collective-permute-start | bytes 98312 | tf_op jit(solution)/shard_map/ppermute | solution.py:191
  589.1 14.0 %collective-permute-start.35 = (bf16[176,2048]{1,0:T(8,128)(2,1)S(1)}, bf16[176,2048]{1,0:T(8,128)(2,1)S(1)}, u32[]{:S(2)}, u32[]{:S(2)}) collective-permute-start(bf16[176,2048]{1,0:T(8,128)(2,1)S(1)} %slice.306), channel_id=1, source_target_pairs={{0,2},{1,3},{2,0},{3,1},{4,6},{5,7},{6,4},{7,5},{8,10},{9,11},{10,... | collective-permute-start | bytes 2162696 | tf_op jit(solution)/shard_map/ppermute | solution.py:191
  591.1 10.7 %collective-permute-start.34 = (bf16[160,2048]{1,0:T(8,128)(2,1)S(1)}, bf16[160,2048]{1,0:T(8,128)(2,1)S(1)}, u32[]{:S(2)}, u32[]{:S(2)}) collective-permute-start(bf16[160,2048]{1,0:T(8,128)(2,1)S(1)} %slice.305), channel_id=1, source_target_pairs={{0,1},{1,0},{2,3},{3,2},{4,5},{5,4},{6,7},{7,6},{8,9},{9,8},{10,11... | collective-permute-start | bytes 1966088 | tf_op jit(solution)/shard_map/ppermute | solution.py:191
  631.4 27.5 %collective-permute-start.40 = (bf16[176,256]{1,0:T(8,128)(2,1)}, bf16[176,256]{1,0:T(8,128)(2,1)}, u32[]{:S(2)}, u32[]{:S(2)}) collective-permute-start(bf16[176,256]{1,0:T(8,128)(2,1)} %slice_bitcast_fusion.9), channel_id=1, source_target_pairs={{0,2},{1,3},{2,0},{3,1},{4,6},{5,7},{6,4},{7,5},{8,10},{9,11},{10,... | collective-permute-start | bytes 270344 | tf_op jit(solution)/shard_map/ppermute | solution.py:191
  635.7 131.8 %reduce-scatter.11.cloned.1.call-start = ((), (), s32[]{:S(2)}) async-start(), calls=%async_computation.9 | async-start | bytes 2654208 | tf_op jit(solution)/shard_map/reduce_scatter | solution.py:417
  635.8 23.1 %collective-permute-start.42 = (bf16[160,256]{1,0:T(8,128)(2,1)S(1)}, bf16[160,256]{1,0:T(8,128)(2,1)}, u32[]{:S(2)}, u32[]{:S(2)}) collective-permute-start(bf16[160,256]{1,0:T(8,128)(2,1)S(1)} %slice_bitcast_fusion.10), channel_id=1, source_target_pairs={{0,1},{1,0},{2,3},{3,2},{4,5},{5,4},{6,7},{7,6},{8,9},{9,8},{10,11... | collective-permute-start | bytes 245768 | tf_op jit(solution)/shard_map/ppermute | solution.py:191
  638.3 19.8 %collective-permute-start.59 = (f32[64,128]{1,0:T(8,128)S(1)}, f32[64,128]{1,0:T(8,128)}, u32[]{:S(2)}, u32[]{:S(2)}) collective-permute-start(f32[64,128]{1,0:T(8,128)S(1)} %add.424), channel_id=1, source_target_pairs={{0,8},{4,12},{8,0},{12,4},{16,24},{20,28},{24,16},{28,20},{1,9},{5... | collective-permute-start | bytes 98312 | tf_op jit(solution)/shard_map/ppermute | solution.py:191
  658.9 6.8 collective-permute-start.60
  660.6 5.8 collective-permute-start.41
  661.1 5.8 collective-permute-start.43
  677.9 6.9 collective-permute-start.49
  678.5 6.3 collective-permute-start.51
  682.8 28.5 %collective-permute-start.36 = (bf16[176,2048]{1,0:T(8,128)(2,1)}, bf16[176,2048]{1,0:T(8,128)(2,1)}, u32[]{:S(2)}, u32[]{:S(2)}) collective-permute-start(bf16[176,2048]{1,0:T(8,128)(2,1)} %slice.307), channel_id=1, source_target_pairs={{0,2},{1,3},{2,0},{3,1},{4,6},{5,7},{6,4},{7,5},{8,10},{9,11},{10,... | collective-permute-start | bytes 2162696 | tf_op jit(solution)/shard_map/ppermute | solution.py:191
  684.2 20.4 %collective-permute-start.38 = (bf16[160,2048]{1,0:T(8,128)(2,1)}, bf16[160,2048]{1,0:T(8,128)(2,1)}, u32[]{:S(2)}, u32[]{:S(2)}) collective-permute-start(bf16[160,2048]{1,0:T(8,128)(2,1)} %slice.308), channel_id=1, source_target_pairs={{0,1},{1,0},{2,3},{3,2},{4,5},{5,4},{6,7},{7,6},{8,9},{9,8},{10,11... | collective-permute-start | bytes 1966088 | tf_op jit(solution)/shard_map/ppermute | solution.py:191
  684.9 19.0 %collective-permute-start.50 = (bf16[512,256]{1,0:T(8,128)(2,1)S(1)}, bf16[512,256]{1,0:T(8,128)(2,1)S(1)}, u32[]{:S(2)}, u32[]{:S(2)}) collective-permute-start(bf16[512,256]{1,0:T(8,128)(2,1)S(1)} %get-tuple-element.71), channel_id=1, source_target_pairs={{0,1},{1,0},{2,3},{3,2},{4,5},{5,4},{6,7},{7,6},{8,9},{9,8},{10,11... | collective-permute-start | bytes 786440 | tf_op jit(solution)/shard_map/ppermute | solution.py:191
  686.4 17.9 %collective-permute-start.52 = (bf16[512,256]{1,0:T(8,128)(2,1)S(1)}, bf16[512,256]{1,0:T(8,128)(2,1)S(1)}, u32[]{:S(2)}, u32[]{:S(2)}) collective-permute-start(bf16[512,256]{1,0:T(8,128)(2,1)S(1)} %get-tuple-element.72), channel_id=1, source_target_pairs={{0,2},{1,3},{2,0},{3,1},{4,6},{5,7},{6,4},{7,5},{8,10},{9,11},{10,... | collective-permute-start | bytes 786440 | tf_op jit(solution)/shard_map/ppermute | solution.py:191
  708.5 29.3 %collective-permute-start.39 = (bf16[336,2048]{1,0:T(8,128)(2,1)}, bf16[336,2048]{1,0:T(8,128)(2,1)}, u32[]{:S(2)}, u32[]{:S(2)}) collective-permute-start(bf16[336,2048]{1,0:T(8,128)(2,1)} %add_convert_fusion), channel_id=1, source_target_pairs={{0,2},{1,3},{2,0},{3,1},{4,6},{5,7},{6,4},{7,5},{8,10},{9,11},{10,... | collective-permute-start | bytes 4128776 | tf_op jit(solution)/shard_map/ppermute | solution.py:191
  715.1 28.8 %collective-permute-start.37 = (bf16[336,2048]{1,0:T(8,128)(2,1)}, bf16[336,2048]{1,0:T(8,128)(2,1)}, u32[]{:S(2)}, u32[]{:S(2)}) collective-permute-start(bf16[336,2048]{1,0:T(8,128)(2,1)} %add_convert_fusion.1), channel_id=1, source_target_pairs={{0,1},{1,0},{2,3},{3,2},{4,5},{5,4},{6,7},{7,6},{8,9},{9,8},{10,11... | collective-permute-start | bytes 4128776 | tf_op jit(solution)/shard_map/ppermute | solution.py:191
  720.7 3.8 collective-permute-start.54
  724.5 5.5 collective-permute-start.55
  747.7 3.8 collective-permute-start.44
  756.6 4.5 collective-permute-start.47
  761.1 4.7 collective-permute-start.48
  (89 other events, 1276.5 us)
Sparse Core Ops, SparseCore 0:
  14.0 51.7 all-gather.8
  67.4 80.7 all-gather.4
  149.8 80.9 all-gather.6
  334.1 103.0 reduce-scatter.4
  440.0 87.9 reduce-scatter.6
  635.8 49.3 reduce-scatter.8
  717.9 38.1 reduce-scatter.10

commit v2 on v1

v2 whole, which is shorter than its diff:
```python
import functools
import math

import jax
import jax.numpy as jnp
from jax import lax
from jax.experimental import pallas as pl
from jax.experimental.pallas import tpu as pltpu
from jax.sharding import PartitionSpec as P

LEN = 1344
HD = 128
QB = 112
KB = 224
SCALE = 1.0 / math.sqrt(HD)
EXP2 = SCALE * math.log2(math.e)
NEG = -1e30
BF = jnp.bfloat16
F32 = jnp.float32


def _stack(ref, heads):
    return jnp.concatenate([ref[0, :, h * HD : (h + 1) * HD] for h in range(heads)], axis=0)


def _allowed(info_ref, first):
    shape = (KB, info_ref.shape[2])
    place = lax.broadcasted_iota(jnp.int32, shape, 0) + first
    return (place >= info_ref[0, 0:1, :]) & (place <= info_ref[0, 1:2, :])


def _nt(a, b):
    return lax.dot_general(a, b, (((1,), (1,)), ((), ())), preferred_element_type=F32)


def _turn(ref, out):
    for c in range(LEN // KB):
        out[c] = ref[0, c * KB : (c + 1) * KB, :].astype(F32).T.astype(BF)


def attend_kernel(
    heads, per_seq, place_ref, low_ref, top_ref, q_ref, k_ref, v_ref, info_ref, o_ref, lse_ref, s_ref, vt_ref
):
    step = pl.program_id(0)
    low, top = low_ref[step], top_ref[step]

    @pl.when(lax.rem(step, per_seq) == 0)
    def _():
        _turn(v_ref, vt_ref)

    q = _stack(q_ref, heads)
    rows = q.shape[0]

    def score(c, best):
        s = _nt(k_ref[0, pl.ds(pl.multiple_of(c * KB, KB), KB), :], q)
        s = jnp.where(_allowed(info_ref, c * KB), s, NEG)
        s_ref[c] = s
        return jnp.maximum(best, jnp.max(s, axis=0, keepdims=True))

    best = lax.fori_loop(low, top, score, jnp.full((1, rows), NEG, F32))
    shift = best * EXP2

    def mix(c, carry):
        total, acc = carry
        p = jnp.exp2(s_ref[c] * EXP2 - shift)
        total = total + jnp.sum(p, axis=0, keepdims=True)
        acc = acc + jnp.dot(vt_ref[c], p.astype(BF), preferred_element_type=F32)
        return total, acc

    total, acc = lax.fori_loop(
        low, top, mix, (jnp.zeros((1, rows), F32), jnp.zeros((HD, rows), F32))
    )
    out = (acc / total).T.astype(BF)
    for h in range(heads):
        o_ref[0, :, h * HD : (h + 1) * HD] = out[h * QB : (h + 1) * QB]
    lse_ref[0] = jnp.broadcast_to(shift + jnp.log2(total), lse_ref.shape[1:])


def attend_back_kernel(
    heads, per_seq, place_ref, low_ref, top_ref, q_ref, o_ref, do_ref, k_ref, v_ref, info_ref, lse_ref,
    dq_ref, dkv_ref, dk_acc, dv_acc, kt_ref,
):
    step = pl.program_id(0)
    inner = lax.rem(step, per_seq)
    low, top = low_ref[step], top_ref[step]

    @pl.when(inner == 0)
    def _():
        dk_acc[...] = jnp.zeros_like(dk_acc)
        dv_acc[...] = jnp.zeros_like(dv_acc)
        _turn(k_ref, kt_ref)

    q = _stack(q_ref, heads)
    do = _stack(do_ref, heads)
    rows = q.shape[0]
    prod = do.astype(F32) * _stack(o_ref, heads).astype(F32)
    delta = jnp.sum(prod.T, axis=0, keepdims=True)
    lse = lse_ref[0, 0:1, :]

    def body(c, acc):
        window = pl.ds(pl.multiple_of(c * KB, KB), KB)
        s = _nt(k_ref[0, window, :], q)
        s = jnp.where(_allowed(info_ref, c * KB), s * EXP2 - lse, NEG)
        p = jnp.exp2(s)
        dp = _nt(v_ref[0, window, :], do)
        ds = (p * (dp - delta)).astype(BF)
        dv_acc[window, :] += jnp.dot(p.astype(BF), do, preferred_element_type=F32)
        dk_acc[window, :] += jnp.dot(ds, q, preferred_element_type=F32)
        return acc + jnp.dot(kt_ref[c], ds, preferred_element_type=F32)

    acc = lax.fori_loop(low, top, body, jnp.zeros((HD, rows), F32))
    dq = (acc * SCALE).T.astype(BF)
    for h in range(heads):
        dq_ref[0, :, h * HD : (h + 1) * HD] = dq[h * QB : (h + 1) * QB]

    @pl.when(inner == per_seq - 1)
    def _():
        dkv_ref[0, :, :HD] = (dk_acc[...] * SCALE).astype(BF)
        dkv_ref[0, :, HD:] = dv_acc[...].astype(BF)


class Attention:
    def __init__(self, segment, place, rows, heads):
        self.heads, self.rows = heads, rows
        self.seqs = segment.shape[0] // LEN
        self.per_seq = LEN // QB
        self.per_block = rows // QB
        self.steps = self.seqs * self.per_seq
        self.place = place
        seg = segment.reshape(self.seqs, LEN)
        start = jnp.sum((seg[:, None, :] < seg[:, :, None]).astype(jnp.int32), axis=-1)
        pos = jnp.broadcast_to(jnp.arange(LEN, dtype=jnp.int32), seg.shape)
        info = jnp.stack([start, pos], axis=1).reshape(self.seqs, 2, self.per_seq, 1, QB)
        info = jnp.broadcast_to(info, (self.seqs, 2, self.per_seq, heads, QB))
        self.info = info.transpose(0, 2, 1, 3, 4).reshape(self.steps, 2, heads * QB)
        self.low = start.reshape(self.steps, QB)[:, 0] // KB
        last = pos.reshape(self.steps, QB)[:, -1]
        self.top = last // KB + 1

    def _specs(self):
        per_seq, per_block, heads = self.per_seq, self.per_block, self.heads
        wide = heads * HD
        query = pl.BlockSpec((1, QB, wide), lambda i, place, *_: (place[i // per_block], i % per_block, 0))
        key = pl.BlockSpec((1, LEN, HD), lambda i, *_: (i // per_seq, 0, 0))
        value = pl.BlockSpec((1, LEN, HD), lambda i, *_: (i // per_seq, 0, 1))
        info = pl.BlockSpec((1, 2, heads * QB), lambda i, *_: (i, 0, 0))
        lse = pl.BlockSpec((1, 8, heads * QB), lambda i, *_: (i, 0, 0))
        return query, key, value, info, lse

    def _cost(self, products):
        pairs = self.steps * QB * self.heads * LEN // 2
        return pl.CostEstimate(
            flops=2 * pairs * HD * products, transcendentals=pairs, bytes_accessed=8 * self.steps * QB * HD * self.heads
        )

    def forward(self, q, keyval):
        query, key, value, info, lse = self._specs()
        lanes = self.heads * QB
        return pl.pallas_call(
            functools.partial(attend_kernel, self.heads, self.per_seq),
            grid_spec=pltpu.PrefetchScalarGridSpec(
                num_scalar_prefetch=3,
                grid=(self.steps,),
                in_specs=[query, key, value, info],
                out_specs=[query, lse],
                scratch_shapes=[pltpu.VMEM((LEN // KB, KB, lanes), F32), pltpu.VMEM((LEN // KB, HD, KB), BF)],
            ),
            out_shape=[
                jax.ShapeDtypeStruct((*q.shape[:2], self.heads * HD), BF),
                jax.ShapeDtypeStruct((self.steps, 8, lanes), F32),
            ],
            cost_estimate=self._cost(2),
            name="attend",
        )(self.place, self.low, self.top, q, keyval, keyval, self.info)

    def backward(self, q, o, do, keyval, lse_in):
        query, key, value, info, lse = self._specs()
        per_seq = self.per_seq
        return pl.pallas_call(
            functools.partial(attend_back_kernel, self.heads, per_seq),
            grid_spec=pltpu.PrefetchScalarGridSpec(
                num_scalar_prefetch=3,
                grid=(self.steps,),
                in_specs=[query, query, query, key, value, info, lse],
                out_specs=[query, pl.BlockSpec((1, LEN, 2 * HD), lambda i, *_: (i // per_seq, 0, 0))],
                scratch_shapes=[
                    pltpu.VMEM((LEN, HD), F32),
                    pltpu.VMEM((LEN, HD), F32),
                    pltpu.VMEM((LEN // KB, HD, KB), BF),
                ],
            ),
            out_shape=[
                jax.ShapeDtypeStruct((*q.shape[:2], self.heads * HD), BF),
                jax.ShapeDtypeStruct((self.seqs, LEN, 2 * HD), BF),
            ],
            cost_estimate=self._cost(5),
            name="attend_back",
        )(self.place, self.low, self.top, q, o, do, keyval, keyval, self.info, lse_in)


def _hop(v, axis, mask):
    size = lax.axis_size(axis)
    return lax.ppermute(v, axis, [(i, i ^ mask) for i in range(size)])


def _half(rows):
    return rows // 2 // 16 * 16


class Square:
    def __init__(self, blocks):
        self.count = blocks
        me = lax.axis_index("tensor")
        self.place = me ^ jnp.arange(blocks, dtype=jnp.int32)

    def near(self, v):
        return _hop(v, "tensor", 1), _hop(v, "tensor", 2)

    def far(self, v, near):
        h = _half(v.shape[0])
        bx, by = near
        top, bottom = _hop(by[:h], "tensor", 1), _hop(bx[h:], "tensor", 2)
        return jnp.concatenate([v, bx, by, top, bottom], axis=0)

    def gather(self, v):
        return self.far(v, self.near(v))

    def gather_small(self, v):
        blocks = jnp.stack([v] + [_hop(v, "tensor", r) for r in range(1, self.count)])
        return self.ordered(blocks)

    def scatter_small(self, parts):
        parts = self.ordered(parts)
        return parts[0] + sum(_hop(parts[r], "tensor", r) for r in range(1, self.count))

    def begin(self, make):
        corner = make(3).astype(BF)
        h = _half(corner.shape[0])
        return _hop(corner[:h], "tensor", 1), _hop(corner[h:], "tensor", 2)

    def middle(self, begun, make):
        to_y, to_x = begun
        rest = to_x.shape[0]
        h = to_y.shape[0]
        zero = [(0, 0)] * (to_x.ndim - 1)
        py = make(2) + jnp.pad(to_y.astype(F32), [(0, rest)] + zero)
        px = make(1) + jnp.pad(to_x.astype(F32), [(h, 0)] + zero)
        return py.astype(BF), px.astype(BF)

    def finish(self, sums, make):
        py, px = sums
        ry, rx = _hop(py, "tensor", 2), _hop(px, "tensor", 1)
        own = make(0)
        return lambda *others: self._end(own, rx, ry, others)

    def _end(self, own, rx, ry, others):
        if others:
            rx, ry = after((rx, ry), *others)
        return own + rx.astype(F32) + ry.astype(F32)

    def scatter(self, make):
        return self.finish(self.middle(self.begin(make), make), make)()

    def ordered(self, stacked):
        return jnp.take(stacked, self.place, axis=0, mode="clip")


class Plain:
    def __init__(self, blocks):
        self.count = blocks
        self.place = jnp.arange(blocks, dtype=jnp.int32)

    def near(self, v):
        return ()

    def far(self, v, near):
        return lax.all_gather(v, "tensor", axis=0, tiled=True)

    def gather(self, v):
        return self.far(v, ())

    def gather_small(self, v):
        return lax.all_gather(v, "tensor", axis=0)

    def scatter_small(self, parts):
        return lax.psum_scatter(parts, "tensor", scatter_dimension=0)

    def begin(self, make):
        return ()

    def middle(self, begun, make):
        return (jnp.concatenate([make(i).astype(BF) for i in range(self.count)], axis=0),)

    def finish(self, sums, make):
        total = lax.psum_scatter(sums[0], "tensor", scatter_dimension=0, tiled=True).astype(F32)
        return lambda *others: total

    def scatter(self, make):
        return self.finish(self.middle((), make), make)()

    def ordered(self, stacked):
        return stacked


def after(value, *others):
    return lax.optimization_barrier((value, others))[0]


def share_kernel(dp, nt, parts_ref, local_ref, sum_ref, local_sum_ref, got, local_got, sent, came, local_sent, local_came):
    me_dp, me_t = lax.axis_index("dp"), lax.axis_index("tensor")
    count = dp * nt
    barrier = pltpu.get_barrier_semaphore()

    def peer(r):
        return lax.rem(me_dp + r // nt, dp), lax.rem(me_t + lax.rem(r, nt), nt)

    def greet(r, _):
        d, t = peer(r)
        pl.semaphore_signal(barrier, inc=1, device_id=(d, t), device_id_type=pl.DeviceIdType.MESH)
        return 0

    lax.fori_loop(1, count, greet, 0)
    pl.semaphore_wait(barrier, count - 1)

    def part_copy(r):
        d, t = peer(r)
        return pltpu.make_async_remote_copy(
            src_ref=parts_ref.at[d * nt + t],
            dst_ref=got.at[r],
            send_sem=sent.at[r],
            recv_sem=came.at[r],
            device_id=(d, t),
            device_id_type=pl.DeviceIdType.MESH,
        )

    def local_copy(a, slot):
        return pltpu.make_async_remote_copy(
            src_ref=local_ref,
            dst_ref=local_got.at[slot],
            send_sem=local_sent.at[a],
            recv_sem=local_came.at[a],
            device_id=(lax.rem(me_dp + a, dp), me_t),
            device_id_type=pl.DeviceIdType.MESH,
        )

    def send(r, _):
        part_copy(r).start()
        return 0

    def send_local(a, _):
        local_copy(a, me_dp).start()
        return 0

    lax.fori_loop(1, dp, send_local, 0)
    lax.fori_loop(1, count, send, 0)
    local_got[me_dp] = local_ref[...]

    def take(r, total):
        part_copy(r).wait()
        return total + got[r]

    sum_ref[...] = lax.fori_loop(1, count, take, parts_ref[me_dp * nt + me_t])

    def take_local(a, _):
        local_copy(a, lax.rem(me_dp + dp - a, dp)).wait()
        return 0

    lax.fori_loop(1, dp, take_local, 0)
    local_sum_ref[...] = jnp.sum(local_got[...], axis=0)


def share_sums(parts, local):
    dp, nt = lax.axis_size("dp"), lax.axis_size("tensor")
    vmem = pl.BlockSpec(memory_space=pltpu.VMEM)
    return pl.pallas_call(
        functools.partial(share_kernel, dp, nt),
        in_specs=[vmem, vmem],
        out_specs=[vmem, vmem],
        out_shape=[jax.ShapeDtypeStruct(parts.shape[1:], F32), jax.ShapeDtypeStruct(local.shape, F32)],
        scratch_shapes=[
            pltpu.VMEM(parts.shape, F32),
            pltpu.VMEM((dp, *local.shape), F32),
            pltpu.SemaphoreType.DMA((dp * nt,)),
            pltpu.SemaphoreType.DMA((dp * nt,)),
            pltpu.SemaphoreType.DMA((dp,)),
            pltpu.SemaphoreType.DMA((dp,)),
        ],
        compiler_params=pltpu.CompilerParams(collective_id=0, has_side_effects=True),
        name="share_sums",
    )(parts, local)


def norm_parts(v):
    average = jnp.mean(v, axis=-1, keepdims=True)
    centered = v - average
    rate = lax.rsqrt(jnp.mean(centered * centered, axis=-1, keepdims=True) + 1e-05)
    return centered * rate, rate


def norm_back(grad, hat, rate, gain):
    scaled = grad * gain
    return rate * (
        scaled
        - jnp.mean(scaled, axis=-1, keepdims=True)
        - hat * jnp.mean(scaled * hat, axis=-1, keepdims=True)
    )


GELU_A = math.sqrt(2.0 / math.pi)
GELU_B = 0.044715


def gelu_both(a):
    square = a * a
    t = jnp.tanh(GELU_A * (a + GELU_B * square * a))
    half = 0.5 * (1.0 + t)
    slope = half + 0.5 * a * (1.0 - t * t) * (GELU_A * (1.0 + 3.0 * GELU_B * square))
    return a * half, slope


def dot(a, b):
    return jnp.dot(a, b, preferred_element_type=F32)


def dot_t(a, b):
    return lax.dot_general(a, b, (((1,), (1,)), ((), ())), preferred_element_type=F32)


def dot_tokens(a, b):
    return lax.dot_general(a, b, (((0,), (0,)), ((), ())), preferred_element_type=F32)


def per_device(
    tokens,
    segment,
    cotangent,
    ln1_gain,
    ln1_shift,
    w_query,
    b_query,
    w_keyval,
    b_value,
    w_out,
    b_out,
    ln2_gain,
    ln2_shift,
    w_in,
    b_in,
    w_back,
    b_back,
):
    dp, nt = lax.axis_size("dp"), lax.axis_size("tensor")
    rows, width = tokens.shape
    heads = b_query.shape[0] // HD
    wide = heads * HD
    inputs = tokens.astype(F32)
    net = Square(nt) if nt == 4 else Plain(nt)

    hat1, rate1 = norm_parts(inputs)
    normed1 = (hat1 * ln1_gain + ln1_shift).astype(BF)
    n1_near = net.near(normed1)

    keyval_rows = net.gather_small(after(w_keyval.astype(BF), normed1)).reshape(w_query.shape[0], 2 * HD)
    pack = jnp.concatenate([w_query.astype(BF), keyval_rows], axis=1)
    first_full = lax.all_gather(pack, "dp", axis=0, tiled=True)
    output_full = lax.all_gather(w_out.astype(BF), "dp", axis=1, tiled=True)
    inner_full = lax.all_gather(w_in.astype(BF), "dp", axis=0, tiled=True)
    down_full = lax.all_gather(w_back.astype(BF), "dp", axis=1, tiled=True)

    n1 = net.far(normed1, n1_near)
    bias = jnp.concatenate([b_query, jnp.zeros_like(b_value), b_value])
    mixed = (dot(n1, first_full) + bias).astype(BF).reshape(nt, rows, -1)
    seqs = nt * rows // LEN
    keyval = net.ordered(mixed[:, :, wide:]).reshape(seqs, LEN, 2 * HD)
    attention = Attention(segment, net.place, rows, heads)
    cot_near = net.near(after(cotangent, n1))
    mixture, lse = attention.forward(mixed, keyval)
    mixture, cot_near = after((mixture, cot_near))
    attended = net.scatter(lambda i: dot(mixture[i], output_full))
    hidden = inputs + attended + b_out

    def block(whole, i):
        return whole[i * rows : (i + 1) * rows]

    hat2, rate2 = norm_parts(hidden)
    normed2 = (hat2 * ln2_gain + ln2_shift).astype(BF)
    n2 = net.gather(normed2)
    cot = net.far(cotangent, after(cot_near, n2))
    act, slope = gelu_both(dot(n2, inner_full) + b_in)
    act, slope = act.astype(BF), slope.astype(BF)
    down_grad = dot_tokens(act, cot).astype(BF)
    down_total = lax.psum_scatter(down_grad, "dp", scatter_dimension=1, tiled=True).astype(F32)
    pre_grad = (dot_t(after(cot, down_grad), down_full) * slope.astype(F32)).astype(BF)
    second_made = lambda i: dot_t(block(pre_grad, i), inner_full)
    second_sums = net.middle(net.begin(second_made), second_made)
    second_end = net.finish(second_sums, second_made)
    inner_grad = dot_tokens(after(n2, second_sums), pre_grad).astype(BF)
    inner_total = lax.psum_scatter(inner_grad, "dp", scatter_dimension=0, tiled=True).astype(F32)
    inner_bias = jnp.sum(pre_grad, axis=0, dtype=F32)
    feed_all = dot(after(act, inner_grad), down_full).astype(BF)
    second_grad = second_end(feed_all)

    grad_out = cotangent.astype(F32)
    hidden_grad = grad_out + norm_back(second_grad, hat2, rate2, ln2_gain)
    hid = net.gather(hidden_grad.astype(BF))
    mixture_grad = dot_t(hid, output_full).astype(BF).reshape(nt, rows, wide)
    feed_made = lambda i: block(feed_all, i).astype(F32)
    feed_all = after(feed_all, hid)
    feed_begun = net.begin(feed_made)
    mixture_grad, feed_begun = after((mixture_grad, feed_begun), down_total)
    feed_end = net.finish(net.middle(feed_begun, feed_made), feed_made)
    query_low, keyval_part = attention.backward(mixed, mixture, mixture_grad, keyval, lse)
    output_grad = dot_tokens(mixture.reshape(nt * rows, wide), hid).astype(BF)
    output_total = lax.psum_scatter(output_grad, "dp", scatter_dimension=1, tiled=True).astype(F32)
    keyval_part = net.ordered(keyval_part.reshape(nt, rows, 2 * HD))
    mixed_grad = jnp.concatenate([query_low, keyval_part], axis=2)
    feed = feed_end(mixed_grad)
    output = (hidden + feed + b_back).astype(BF)
    mixed_grad = after(mixed_grad, output, inner_total)
    normed_made = lambda i: dot_t(mixed_grad[i], first_full)
    first_grad = dot_tokens(n1, mixed_grad.reshape(nt * rows, -1)).astype(BF)
    first_bias = jnp.sum(mixed_grad, axis=(0, 1), dtype=F32)
    first_total = lax.psum_scatter(first_grad, "dp", scatter_dimension=0, tiled=True)
    query_total = first_total[:, :wide].astype(F32)
    keyval_total = net.scatter_small(first_total[:, wide:].reshape(nt, w_keyval.shape[0], 2 * HD)).astype(F32)
    normed_grad = net.scatter(normed_made)
    tokens_grad = (hidden_grad + norm_back(normed_grad, hat1, rate1, ln1_gain)).astype(BF)

    count = dp * nt
    wide_sums = jnp.stack(
        [
            jnp.sum(normed_grad * hat1, axis=0),
            jnp.sum(normed_grad, axis=0),
            jnp.sum(second_grad * hat2, axis=0),
            jnp.sum(second_grad, axis=0),
            jnp.sum(hidden_grad, axis=0),
            jnp.sum(grad_out, axis=0),
        ]
    )
    kinds, part, value_part = wide_sums.shape[0], width // count, HD // count
    parts = wide_sums.reshape(kinds, count, part).transpose(1, 0, 2).reshape(count, kinds * part)
    parts = jnp.concatenate([parts, first_bias[wide + HD :].reshape(count, value_part)], axis=1)
    lines = pl.cdiv(parts.shape[1], 128)
    parts = jnp.pad(parts, ((0, 0), (0, lines * 128 - parts.shape[1]))).reshape(count, lines, 128)
    local = jnp.concatenate([inner_bias, first_bias[:wide]]).reshape(-1, 128)
    sums, local = share_sums(parts, local)
    sums, local = sums.reshape(-1), local.reshape(-1)
    value_bias = sums[kinds * part : kinds * part + value_part]
    sums = sums[: kinds * part].reshape(kinds, part)
    return (
        output,
        tokens_grad,
        sums[0],
        sums[1],
        query_total,
        local[b_in.shape[0] :],
        keyval_total,
        value_bias,
        output_total,
        sums[4],
        sums[2],
        sums[3],
        inner_total,
        local[: b_in.shape[0]],
        down_total,
        sums[5],
    )


def solution(mesh):
    return jax.shard_map(
        per_device,
        mesh=mesh,
        in_specs=(
            P(("dp", "tensor"), None),
            P("dp"),
            P(("dp", "tensor"), None),
            P(),
            P(),
            P("dp", "tensor"),
            P("tensor"),
            P(("dp", "tensor"), None),
            P(),
            P("tensor", "dp"),
            P(),
            P(),
            P(),
            P("dp", "tensor"),
            P("tensor"),
            P("tensor", "dp"),
            P(),
        ),
        out_specs=(
            P(("dp", "tensor"), None),
            P(("dp", "tensor"), None),
            P(("dp", "tensor")),
            P(("dp", "tensor")),
            P("dp", "tensor"),
            P("tensor"),
            P(("dp", "tensor"), None),
            P(("dp", "tensor")),
            P("tensor", "dp"),
            P(("dp", "tensor")),
            P(("dp", "tensor")),
            P(("dp", "tensor")),
            P("dp", "tensor"),
            P("tensor"),
            P("tensor", "dp"),
            P(("dp", "tensor")),
        ),
        check_vma=False,
    )
```

time: 789 us -> 607 us (0.77)
  waiting for transfers between devices: 327 us -> 211 us
  starting transfers between devices: 90.2 us -> 43 us
  local copies, waits for them, and re-layouts: 80.1 us -> 46.8 us
  Pallas kernels: 34.6 us -> 55.2 us
    ppermute x61 -> x38, waiting for transfers between devices: 279 us -> 211 us  [_hop(): return lax.ppermute(v, axis, [(i, i ^ mask) for i in range(size)])]
    reduce_scatter x1, waiting for transfers between devices: 47.5 us -> 0.01 us  [per_device(): lax.psum_scatter(down_grad, 'dp', scatter_dimension=1, tiled=True)]
    ppermute x61 -> x38, starting transfers between devices: 89.8 us -> 42.7 us  [_hop(): return lax.ppermute(v, axis, [(i, i ^ mask) for i in range(size)])]
    pallas_call x1 -> x2, Pallas kernels: 16.2 us -> 36.9 us  [the longest x1 21 us: share_sums(): pl.pallas_call(functools.partial(share_kernel, dp, nt), in_specs=[vmem, v...]
    slice x30 -> x21, local copies, waits for them, and re-layouts: 17.3 us -> 8.51 us  [the longest x8 5.03 us: far(): top, bottom = (_hop(by[:h], 'tensor', 1), _hop(bx[h:], 'tensor', 2))]
    convert_element_type x10 -> x9, other arithmetic: 12.4 us -> 19.6 us  [the longest x1 4.55 us: middle(): return (py.astype(BF), px.astype(BF))]
    unnamed x183 -> x112, local copies, waits for them, and re-layouts: 29.2 us -> 23.1 us
    dot_general x17 -> x10, matrix products: 75.9 us -> 73.2 us  [dot_t(): lax.dot_general(a, b, (((1,), (1,)), ((), ())), preferred_element_type=F32)]
  transfers between devices with their start and end apart: 68 -> 46, of which waited for: 43 -> 28; matrix products, arithmetic and copies ran while one was open for 37% -> 42% of each run, Pallas kernels for 4% -> 9%
where the time goes in v2:
time: 607 us; the launch traced here: 596 us
  waiting for transfers between devices  211 us (35%)
  matrix products  170 us (28%)
  Pallas kernels  55.2 us (9%)
  other arithmetic  54.8 us (9%)
  local copies, waits for them, and re-layouts  46.8 us (8%)
  starting transfers between devices  43 us (7%)
  between operations  15.2 us (3%)
    ppermute x38, waiting for transfers between devices, _hop(): return lax.ppermute(v, axis, [(i, i ^ mask) for i in range(size)])  211 us
    dot_general x10, matrix products, dot_t(): lax.dot_general(a, b, (((1,), (1,)), ((), ())), preferred_element_type=F32)  73.2 us
    dot_general x7, matrix products, dot(): return jnp.dot(a, b, preferred_element_type=F32)  50 us
    dot_general x4, matrix products, dot_tokens(): lax.dot_general(a, b, (((0,), (0,)), ((), ())), preferred_element_type=F32)  46.9 us
    ppermute x38, starting transfers between devices, _hop(): return lax.ppermute(v, axis, [(i, i ^ mask) for i in range(size)])  42.7 us
    unnamed x112, local copies, waits for them, and re-layouts  23.1 us
    pallas_call x1, Pallas kernels, share_sums(): pl.pallas_call(functools.partial(share_kernel, dp, nt), in_specs=[vmem, v...  21 us
    pallas_call x1, Pallas kernels, backward(): pl.pallas_call(functools.partial(attend_back_kernel, self.heads, per_seq)...  18.3 us
  transfers between devices with their start and end apart: 46, of which 28 were waited for; matrix products, arithmetic and copies ran while one was open for 42% of the time, Pallas kernels for 9%

profile of v2, /device:TPU:0, one launch (start us, length us, event | category | flops | bytes accessed | tf_op | source)
XLA Modules:
  0.0 596.1 jit_solution(3715086231712663499)
XLA Ops:
  9.0 1.9 fusion.16
  11.4 2.2 constant_dynamic-update-slice_fusion.4
  13.6 3.9 collective-permute-start.6
  23.5 2.1 gather_fusion
  25.6 1.8 pad_maximum_fusion
  32.7 2.7 convert_element_type.205
  37.1 24.1 %collective-permute-done.1 = bf16[336,2048]{1,0:T(8,128)(2,1)} collective-permute-done((bf16[336,2048]{1,0:T(8,128)(2,1)}, bf16[336,2048]{1,0:T(8,128)(2,1)}, u32[]{:S(2)}, u32[]{:S(2)}) %collective-permute-start.1) | collective-permute-done | bytes 1376288 | tf_op jit(solution)/shard_map/ppermute | solution.py:203
  61.3 2.0 slice.239
  67.9 2.7 constant_dynamic-update-slice_fusion.2
  70.6 6.8 %collective-permute-done.2 = bf16[160,2048]{1,0:T(8,128)(2,1)S(1)} collective-permute-done((bf16[160,2048]{1,0:T(8,128)(2,1)}, bf16[160,2048]{1,0:T(8,128)(2,1)S(1)}, u32[]{:S(2)}, u32[]{:S(2)}) %collective-permute-start.2) | collective-permute-done | bytes 655392 | tf_op jit(solution)/shard_map/ppermute | solution.py:203
  78.3 2.6 collective-permute-done.3
  85.3 8.0 %add_convert_fusion.1 = bf16[1344,768]{1,0:T(8,128)(2,1)S(1)} fusion(bf16[1344,2048]{1,0:T(8,128)(2,1)} %constant_dynamic-update-slice_fusion, bf16[2048,768]{1,0:T(8,128)(2,1)} %all-gather.5.cloned.1.call-done, f32[768]{0:T(1024)S(1)} %pad_maximum_fusion.2), kind=kOutput, calls=%fused_computation.17 | convolution fusion | flops 4229922816 | bytes 10718208 | tf_op jit(solution)/shard_map/dot_general | solution.py:422
  96.1 15.9 %attend.1 = (bf16[4,336,512]{2,1,0:T(8,128)(2,1)}, f32[12,8,448]{2,1,0:T(8,128)}) custom-call(s32[4]{0:T(128)} %iota_xor_fusion.place_ref, s32[12]{0:T(128)} %get-tuple-element.102.low_ref, s32[12]{0:T(128)} %get-tuple-element.103.top_ref, bf16[4,336,768]{2,1,0:T(8,128)(2,1)} %bitcast.126, bf16[1,1344,256]{2,1,0:T(8,128)(2,1)} %bitcast.113, ...), custom_call_target="tpu_custom_call" | custom-call | flops 1849688064 | bytes 5505024 | tf_op jit(solution)/shard_map/attend/pallas_call | solution.py:159
  112.0 2.7 convolution_convert_fusion.8
  116.3 13.1 %collective-permute-done.11 = bf16[160,2048]{1,0:T(8,128)(2,1)S(1)} collective-permute-done((bf16[160,2048]{1,0:T(8,128)(2,1)S(1)}, bf16[160,2048]{1,0:T(8,128)(2,1)S(1)}, u32[]{:S(2)}, u32[]{:S(2)}) %collective-permute-start.11) | collective-permute-done | bytes 655392 | tf_op jit(solution)/shard_map/ppermute | solution.py:203
  133.1 2.3 collective-permute-start.10
  136.2 24.4 %collective-permute-done.12 = bf16[336,2048]{1,0:T(8,128)(2,1)S(1)} collective-permute-done((bf16[336,2048]{1,0:T(8,128)(2,1)S(1)}, bf16[336,2048]{1,0:T(8,128)(2,1)S(1)}, u32[]{:S(2)}, u32[]{:S(2)}) %collective-permute-start.12) | collective-permute-done | bytes 1376288 | tf_op jit(solution)/shard_map/ppermute | solution.py:203
  163.7 2.0 collective-permute-start.14
  166.0 27.2 %collective-permute-done.14 = bf16[336,2048]{1,0:T(8,128)(2,1)S(1)} collective-permute-done((bf16[336,2048]{1,0:T(8,128)(2,1)S(1)}, bf16[336,2048]{1,0:T(8,128)(2,1)S(1)}, u32[]{:S(2)}, u32[]{:S(2)}) %collective-permute-start.14) | collective-permute-done | bytes 1376288 | tf_op jit(solution)/shard_map/ppermute | solution.py:203
  193.3 2.4 collective-permute-start.15
  197.1 11.6 %collective-permute-done.15 = bf16[160,2048]{1,0:T(8,128)(2,1)S(1)} collective-permute-done((bf16[160,2048]{1,0:T(8,128)(2,1)S(1)}, bf16[160,2048]{1,0:T(8,128)(2,1)S(1)}, u32[]{:S(2)}, u32[]{:S(2)}) %collective-permute-start.15) | collective-permute-done | bytes 655392 | tf_op jit(solution)/shard_map/ppermute | solution.py:203
  216.1 2.6 constant_dynamic-update-slice_fusion.13
  218.7 2.6 constant_dynamic-update-slice_fusion.12
  221.3 3.6 collective-permute-done.17
  225.8 3.6 collective-permute-done.18
  230.3 21.0 %multiply_convert_fusion.1 = (bf16[1344,2048]{1,0:T(8,128)(2,1)S(1)}, f32[1344,2048]{1,0:T(8,128)}) fusion(f32[2048]{0:T(1024)S(1)} %copy-done.40, bf16[1344,2048]{1,0:T(8,128)(2,1)} %copy-done.10, bf16[2048,2048]{1,0:T(8,128)(2,1)} %all-gather.9.cloned.1.call-done), kind=kOutput, calls=%fused_computation.10 | convolution fusion | flops 11301814272 | bytes 30416896 | tf_op jit(solution)/shard_map/dot_general | solution.py:422
  251.3 2.3 copy-done.42
  253.6 18.2 %convolution_convert_fusion.2 = bf16[2048,2048]{1,0:T(8,128)(2,1)} fusion(bf16[1344,2048]{1,0:T(8,128)(2,1)S(1)} %get-tuple-element.51, bf16[1344,2048]{1,0:T(8,128)(2,1)} %constant_dynamic-update-slice_fusion.10), kind=kOutput, calls=%fused_computation.15 | convolution fusion | flops 11278483456 | bytes 19398656 | tf_op jit(solution)/shard_map/dot_general | solution.py:430
  271.9 24.9 %convert_reduce_fusion = (f32[2048]{0:T(1024)S(1)}, bf16[1344,2048]{1,0:T(8,128)(2,1)}) fusion(f32[1344,2048]{1,0:T(8,128)} %get-tuple-element.99, f32[2048]{0:T(1024)S(1)} %copy-done.40, bf16[1344,2048]{1,0:T(8,128)(2,1)} %constant_dynamic-update-slice_fusion.10, bf16[2048,2048]{1,0:T(8,128)(2,1)} %all-gather.11.cloned.1.call-done), kind=kOutput, calls=%fused_computation.7 | convolution fusion | flops 11337594880 | bytes 30425088 | tf_op jit(solution)/shard_map/dot_general | solution.py:426
  296.8 7.1 %convolution_convert_fusion.7 = bf16[336,2048]{1,0:T(8,128)(2,1)S(1)} fusion(bf16[2048,2048]{1,0:T(8,128)(2,1)} %all-gather.9.cloned.1.call-done, bf16[1344,2048]{1,0:T(8,128)(2,1)} %get-tuple-element.101), kind=kOutput, calls=%fused_computation.58 | convolution fusion | flops 2819260416 | bytes 11141120 | tf_op jit(solution)/shard_map/dot_general | solution.py:426
  306.0 10.0 %collective-permute-done.19 = bf16[160,2048]{1,0:T(8,128)(2,1)S(1)} collective-permute-done((bf16[160,2048]{1,0:T(8,128)(2,1)S(1)}, bf16[160,2048]{1,0:T(8,128)(2,1)S(1)}, u32[]{:S(2)}, u32[]{:S(2)}) %collective-permute-start.19) | collective-permute-done | bytes 655392 | tf_op jit(solution)/shard_map/ppermute | solution.py:203
  316.0 10.6 %add_convert_fusion.8 = bf16[336,2048]{1,0:T(8,128)(2,1)} fusion(bf16[160,2048]{1,0:T(8,128)(2,1)S(1)} %collective-permute-done.19, bf16[2048,2048]{1,0:T(8,128)(2,1)} %all-gather.9.cloned.1.call-done, bf16[1344,2048]{1,0:T(8,128)(2,1)S(1)} %copy-done.41), kind=kOutput, calls=%fused_computation.52 | convolution fusion | flops 2820636672 | bytes 11796480 | tf_op jit(solution)/shard_map/dot_general | solution.py:426
  326.6 4.2 add_convert_fusion.7
  330.7 15.8 %convolution_convert_fusion.1 = bf16[2048,2048]{1,0:T(8,128)(2,1)} fusion(bf16[1344,2048]{1,0:T(8,128)(2,1)S(1)} %bitcast.124, bf16[1344,2048]{1,0:T(8,128)(2,1)S(1)} %copy-done.41), kind=kOutput, calls=%fused_computation.14 | convolution fusion | flops 11278483456 | bytes 19398656 | tf_op jit(solution)/shard_map/dot_general | solution.py:430
  346.7 6.6 %fusion.18 = f32[336,2048]{1,0:T(8,128)S(1)} fusion(bf16[2048,2048]{1,0:T(8,128)(2,1)} %all-gather.9.cloned.1.call-done, bf16[1344,2048]{1,0:T(8,128)(2,1)} %get-tuple-element.101), kind=kOutput, calls=%fused_computation.63 | convolution fusion | flops 2818572288 | bytes 12517376 | tf_op jit(solution)/shard_map/dot_general | solution.py:426
  353.3 2.8 collective-permute-start.22
  356.4 15.7 %convolution_convert_fusion = bf16[1344,2048]{1,0:T(8,128)(2,1)S(1)} fusion(bf16[1344,2048]{1,0:T(8,128)(2,1)} %copy-done.42, bf16[2048,2048]{1,0:T(8,128)(2,1)} %all-gather.11.cloned.1.call-done), kind=kOutput, calls=%fused_computation.13 | convolution fusion | flops 11277041664 | bytes 19398656 | tf_op jit(solution)/shard_map/dot_general | solution.py:422
  372.1 10.1 %collective-permute-done.22 = bf16[336,2048]{1,0:T(8,128)(2,1)S(1)} collective-permute-done((bf16[336,2048]{1,0:T(8,128)(2,1)S(1)}, bf16[336,2048]{1,0:T(8,128)(2,1)S(1)}, u32[]{:S(2)}, u32[]{:S(2)}) %collective-permute-start.22) | collective-permute-done | bytes 1376288 | tf_op jit(solution)/shard_map/ppermute | solution.py:203
  389.1 29.1 %collective-permute-done.24 = bf16[336,2048]{1,0:T(8,128)(2,1)S(1)} collective-permute-done((bf16[336,2048]{1,0:T(8,128)(2,1)S(1)}, bf16[336,2048]{1,0:T(8,128)(2,1)S(1)}, u32[]{:S(2)}, u32[]{:S(2)}) %collective-permute-start.24) | collective-permute-done | bytes 1376288 | tf_op jit(solution)/shard_map/ppermute | solution.py:203
  419.3 1.9 collective-permute-start.26
  421.5 10.2 %collective-permute-done.25 = bf16[160,2048]{1,0:T(8,128)(2,1)S(1)} collective-permute-done((bf16[160,2048]{1,0:T(8,128)(2,1)S(1)}, bf16[160,2048]{1,0:T(8,128)(2,1)S(1)}, u32[]{:S(2)}, u32[]{:S(2)}) %collective-permute-start.25) | collective-permute-done | bytes 655392 | tf_op jit(solution)/shard_map/ppermute | solution.py:203
  436.0 4.7 convolution_convert_fusion.5
  440.7 7.4 %convolution_convert_fusion.4 = bf16[1344,512]{1,0:T(8,128)(2,1)} fusion(bf16[1344,2048]{1,0:T(8,128)(2,1)} %copy-done.11, bf16[512,2048]{1,0:T(8,128)(2,1)} %all-gather.7.cloned.1.call-done), kind=kOutput, calls=%fused_computation.30 | convolution fusion | flops 2819260416 | bytes 8978432 | tf_op jit(solution)/shard_map/dot_general | solution.py:426
  448.1 2.7 convert_element_type.221
  450.8 4.6 add_convert_fusion.5
  457.5 18.3 %attend_back.1 = (bf16[4,336,512]{2,1,0:T(8,128)(2,1)}, bf16[1,1344,256]{2,1,0:T(8,128)(2,1)}) custom-call(s32[4]{0:T(128)} %iota_xor_fusion.place_ref, s32[12]{0:T(128)} %get-tuple-element.102.low_ref, s32[12]{0:T(128)} %get-tuple-element.103.top_ref, bf16[4,336,768]{2,1,0:T(8,128)(2,1)} %bitcast.127, bf16[4,336,512]{2,1,0:T(8,128)(2,1)} %get-tuple-element.44.o_ref, ...), custom_call_target="tpu_custom_call" | custom-call | flops 4624220160 | bytes 5505024 | tf_op jit(solution)/shard_map/attend_back/pallas_call | solution.py:179
  475.7 1.8 gather_fusion.2
  477.6 2.6 constant_dynamic-update-slice_fusion.21
  481.1 2.9 convert_element_type.228
  484.1 4.3 add_convert_fusion.4
  488.4 8.3 %convolution_convert_fusion.3 = bf16[2048,768]{1,0:T(8,128)(2,1)} fusion(bf16[1344,2048]{1,0:T(8,128)(2,1)S(1)} %bitcast.122, bf16[1344,768]{1,0:T(8,128)(2,1)} %bitcast.24), kind=kOutput, calls=%fused_computation.23 | convolution fusion | flops 4229431296 | bytes 10715136 | tf_op jit(solution)/shard_map/dot_general | solution.py:430
  496.7 1.9 copy-done.36
  498.6 2.3 convolution_convert_fusion.6
  503.1 8.5 %collective-permute-done.33 = bf16[160,2048]{1,0:T(8,128)(2,1)S(1)} collective-permute-done((bf16[160,2048]{1,0:T(8,128)(2,1)S(1)}, bf16[160,2048]{1,0:T(8,128)(2,1)S(1)}, u32[]{:S(2)}, u32[]{:S(2)}) %collective-permute-start.33) | collective-permute-done | bytes 655392 | tf_op jit(solution)/shard_map/ppermute | solution.py:203
  511.6 3.4 add_convert_fusion.2
  515.1 1.8 collective-permute-start.34
  518.1 3.4 add_convert_fusion.3
  524.0 2.0 convert_reduce_fusion.2
  526.7 3.4 fusion.34
  530.2 13.2 %collective-permute-done.34 = bf16[336,2048]{1,0:T(8,128)(2,1)S(1)} collective-permute-done((bf16[336,2048]{1,0:T(8,128)(2,1)}, bf16[336,2048]{1,0:T(8,128)(2,1)S(1)}, u32[]{:S(2)}, u32[]{:S(2)}) %collective-permute-start.34) | collective-permute-done | bytes 1376288 | tf_op jit(solution)/shard_map/ppermute | solution.py:203
  543.8 4.4 fusion.15
  549.2 21.0 %share_sums.1 = (f32[4,128]{1,0:T(4,128)}, f32[20,128]{1,0:T(8,128)}) custom-call(f32[32,4,128]{2,1,0:T(4,128)} %reshape.263.parts_ref, f32[20,128]{1,0:T(8,128)} %maximum_bitcast_fusion.local_ref), custom_call_target="tpu_custom_call" | custom-call | tf_op jit(solution)/shard_map/share_sums/pallas_call | solution.py:375
  575.2 4.7 fusion.14
  585.1 1.8 slice_convert_fusion
  (273 shorter events, 86.7 us)
Async XLA Ops:
  7.2 78.0 %all-gather.5.cloned.1.call-start = ((), (), s32[]{:S(2)}) async-start(), calls=%async_computation.4 | async-start | bytes 3538944 | tf_op jit(solution)/shard_map/all_gather | solution.py:465
  13.6 15.7 %copy-start.8 = (f32[256,2048]{1,0:T(8,128)S(1)}, f32[256,2048]{1,0:T(8,128)}, u32[]{:S(2)}) copy-start(f32[256,2048]{1,0:T(8,128)} %param.30) | copy-start | bytes 6291460
  13.6 6.3 %collective-permute-start.6 = (bf16[64,256]{1,0:T(8,128)(2,1)S(1)}, bf16[64,256]{1,0:T(8,128)(2,1)S(1)}, u32[]{:S(2)}, u32[]{:S(2)}) collective-permute-start(bf16[64,256]{1,0:T(8,128)(2,1)S(1)} %convert_element_type.193), channel_id=1, source_target_pairs={{0,3},{1,2},{2,1},{3,0},{4,7},{5,6},{6,5},{7,4},{8,11},{9,10},{10,... | collective-permute-start | bytes 98312 | tf_op jit(solution)/shard_map/ppermute | solution.py:203
  17.6 4.0 collective-permute-start.5
  18.1 4.0 collective-permute-start.4
  18.1 76.5 %copy-start.29 = (s32[1024]{0:T(1024)}, s32[1024]{0:T(1024)S(1)}, u32[]{:S(2)}) copy-start(s32[1024]{0:T(1024)S(1)} %pad_clamp_fusion) | copy-start | bytes 12292
  27.5 84.6 %all-gather.7.cloned.1.call-start = ((), (), s32[]{:S(2)}) async-start(), calls=%async_computation.5 | async-start | bytes 2359296 | tf_op jit(solution)/shard_map/all_gather | solution.py:466
  29.3 201.0 %all-gather.9.cloned.1.call-start = ((), (), s32[]{:S(2)}) async-start(), calls=%async_computation.6 | async-start | bytes 9437184 | tf_op jit(solution)/shard_map/all_gather | solution.py:467
  30.5 34.6 %copy-start.34 = (f32[512]{0:T(512)S(1)}, f32[512]{0:T(512)}, u32[]{:S(2)}) copy-start(f32[512]{0:T(512)} %param.23) | copy-start | bytes 6148
  30.5 34.6 %copy-start.35 = (f32[128]{0:T(128)S(1)}, f32[128]{0:T(128)}, u32[]{:S(2)}) copy-start(f32[128]{0:T(128)} %param.25) | copy-start | bytes 1540
  30.5 241.4 %all-gather.11.cloned.1.call-start = ((), (), s32[]{:S(2)}) async-start(), calls=%async_computation.7 | async-start | bytes 9437184 | tf_op jit(solution)/shard_map/all_gather | solution.py:468
  30.6 30.7 %collective-permute-start.1 = (bf16[336,2048]{1,0:T(8,128)(2,1)}, bf16[336,2048]{1,0:T(8,128)(2,1)}, u32[]{:S(2)}, u32[]{:S(2)}) collective-permute-start(bf16[336,2048]{1,0:T(8,128)(2,1)} %get-tuple-element.85), channel_id=1, source_target_pairs={{0,2},{1,3},{2,0},{3,1},{4,6},{5,7},{6,4},{7,5},{8,10},{9,11},{10,... | collective-permute-start | bytes 4128776 | tf_op jit(solution)/shard_map/ppermute | solution.py:203
  32.2 33.0 %collective-permute-start = (bf16[336,2048]{1,0:T(8,128)(2,1)}, bf16[336,2048]{1,0:T(8,128)(2,1)S(1)}, u32[]{:S(2)}, u32[]{:S(2)}) collective-permute-start(bf16[336,2048]{1,0:T(8,128)(2,1)} %get-tuple-element.85), channel_id=1, source_target_pairs={{0,1},{1,0},{2,3},{3,2},{4,5},{5,4},{6,7},{7,6},{8,9},{9,8},{10,11... | collective-permute-start | bytes 4128776 | tf_op jit(solution)/shard_map/ppermute | solution.py:203
  35.4 412.7 %reduce-scatter.5.cloned.1.call-start = ((), (), s32[]{:S(2)}) async-start(), calls=%async_computation.8 | async-start | bytes 9437184 | tf_op jit(solution)/shard_map/reduce_scatter | solution.py:492
  63.2 14.2 %collective-permute-start.2 = (bf16[160,2048]{1,0:T(8,128)(2,1)}, bf16[160,2048]{1,0:T(8,128)(2,1)S(1)}, u32[]{:S(2)}, u32[]{:S(2)}) collective-permute-start(bf16[160,2048]{1,0:T(8,128)(2,1)} %slice.239), channel_id=1, source_target_pairs={{0,1},{1,0},{2,3},{3,2},{4,5},{5,4},{6,7},{7,6},{8,9},{9,8},{10,11... | collective-permute-start | bytes 1966088 | tf_op jit(solution)/shard_map/ppermute | solution.py:203
  65.2 15.7 %collective-permute-start.3 = (bf16[176,2048]{1,0:T(8,128)(2,1)S(1)}, bf16[176,2048]{1,0:T(8,128)(2,1)S(1)}, u32[]{:S(2)}, u32[]{:S(2)}) collective-permute-start(bf16[176,2048]{1,0:T(8,128)(2,1)S(1)} %slice.240), channel_id=1, source_target_pairs={{0,2},{1,3},{2,0},{3,1},{4,6},{5,7},{6,4},{7,5},{8,10},{9,11},{10,... | collective-permute-start | bytes 2162696 | tf_op jit(solution)/shard_map/ppermute | solution.py:203
  81.9 30.1 %collective-permute-start.8 = (bf16[336,2048]{1,0:T(8,128)(2,1)S(1)}, bf16[336,2048]{1,0:T(8,128)(2,1)}, u32[]{:S(2)}, u32[]{:S(2)}) collective-permute-start(bf16[336,2048]{1,0:T(8,128)(2,1)S(1)} %copy-done.5), channel_id=1, source_target_pairs={{0,2},{1,3},{2,0},{3,1},{4,6},{5,7},{6,4},{7,5},{8,10},{9,11},{10,... | collective-permute-start | bytes 4128776 | tf_op jit(solution)/shard_map/ppermute | solution.py:203
  83.1 28.9 %collective-permute-start.7 = (bf16[336,2048]{1,0:T(8,128)(2,1)S(1)}, bf16[336,2048]{1,0:T(8,128)(2,1)}, u32[]{:S(2)}, u32[]{:S(2)}) collective-permute-start(bf16[336,2048]{1,0:T(8,128)(2,1)S(1)} %copy-done.5), channel_id=1, source_target_pairs={{0,1},{1,0},{2,3},{3,2},{4,5},{5,4},{6,7},{7,6},{8,9},{9,8},{10,11... | collective-permute-start | bytes 4128776 | tf_op jit(solution)/shard_map/ppermute | solution.py:203
  112.0 17.4 %copy-start.13 = (bf16[4,336,512]{2,1,0:T(8,128)(2,1)S(1)}, bf16[4,336,512]{2,1,0:T(8,128)(2,1)}, u32[]{:S(2)}) copy-start(bf16[4,336,512]{2,1,0:T(8,128)(2,1)} %get-tuple-element.44.o_ref) | copy-start | bytes 4128772
  114.8 14.6 %collective-permute-start.11 = (bf16[160,2048]{1,0:T(8,128)(2,1)S(1)}, bf16[160,2048]{1,0:T(8,128)(2,1)S(1)}, u32[]{:S(2)}, u32[]{:S(2)}) collective-permute-start(bf16[160,2048]{1,0:T(8,128)(2,1)S(1)} %slice.243), channel_id=1, source_target_pairs={{0,1},{1,0},{2,3},{3,2},{4,5},{5,4},{6,7},{7,6},{8,9},{9,8},{10,11... | collective-permute-start | bytes 1966088 | tf_op jit(solution)/shard_map/ppermute | solution.py:203
  115.9 16.3 %collective-permute-start.9 = (bf16[176,2048]{1,0:T(8,128)(2,1)S(1)}, bf16[176,2048]{1,0:T(8,128)(2,1)S(1)}, u32[]{:S(2)}, u32[]{:S(2)}) collective-permute-start(bf16[176,2048]{1,0:T(8,128)(2,1)S(1)} %slice.242), channel_id=1, source_target_pairs={{0,2},{1,3},{2,0},{3,1},{4,6},{5,7},{6,4},{7,5},{8,10},{9,11},{10,... | collective-permute-start | bytes 2162696 | tf_op jit(solution)/shard_map/ppermute | solution.py:203
  130.3 30.3 %collective-permute-start.12 = (bf16[336,2048]{1,0:T(8,128)(2,1)S(1)}, bf16[336,2048]{1,0:T(8,128)(2,1)S(1)}, u32[]{:S(2)}, u32[]{:S(2)}) collective-permute-start(bf16[336,2048]{1,0:T(8,128)(2,1)S(1)} %add_convert_fusion.10), channel_id=1, source_target_pairs={{0,2},{1,3},{2,0},{3,1},{4,6},{5,7},{6,4},{7,5},{8,10},{9,11},{10,... | collective-permute-start | bytes 4128776 | tf_op jit(solution)/shard_map/ppermute | solution.py:203
  133.0 28.1 %copy-start.31 = (f32[2048]{0:T(1024)S(1)}, f32[2048]{0:T(1024)}, u32[]{:S(2)}) copy-start(f32[2048]{0:T(1024)} %param.27) | copy-start | bytes 24580
  133.1 28.1 %collective-permute-start.10 = (bf16[336,2048]{1,0:T(8,128)(2,1)S(1)}, bf16[336,2048]{1,0:T(8,128)(2,1)S(1)}, u32[]{:S(2)}, u32[]{:S(2)}) collective-permute-start(bf16[336,2048]{1,0:T(8,128)(2,1)S(1)} %add_convert_fusion.11), channel_id=1, source_target_pairs={{0,1},{1,0},{2,3},{3,2},{4,5},{5,4},{6,7},{7,6},{8,9},{9,8},{10,11... | collective-permute-start | bytes 4128776 | tf_op jit(solution)/shard_map/ppermute | solution.py:203
  163.7 29.5 %collective-permute-start.14 = (bf16[336,2048]{1,0:T(8,128)(2,1)S(1)}, bf16[336,2048]{1,0:T(8,128)(2,1)S(1)}, u32[]{:S(2)}, u32[]{:S(2)}) collective-permute-start(bf16[336,2048]{1,0:T(8,128)(2,1)S(1)} %get-tuple-element.81), channel_id=1, source_target_pairs={{0,2},{1,3},{2,0},{3,1},{4,6},{5,7},{6,4},{7,5},{8,10},{9,11},{10,... | collective-permute-start | bytes 4128776 | tf_op jit(solution)/shard_map/ppermute | solution.py:203
  165.7 30.4 %collective-permute-start.13 = (bf16[336,2048]{1,0:T(8,128)(2,1)S(1)}, bf16[336,2048]{1,0:T(8,128)(2,1)S(1)}, u32[]{:S(2)}, u32[]{:S(2)}) collective-permute-start(bf16[336,2048]{1,0:T(8,128)(2,1)S(1)} %get-tuple-element.81), channel_id=1, source_target_pairs={{0,1},{1,0},{2,3},{3,2},{4,5},{5,4},{6,7},{7,6},{8,9},{9,8},{10,11... | collective-permute-start | bytes 4128776 | tf_op jit(solution)/shard_map/ppermute | solution.py:203
  193.3 15.5 %collective-permute-start.15 = (bf16[160,2048]{1,0:T(8,128)(2,1)S(1)}, bf16[160,2048]{1,0:T(8,128)(2,1)S(1)}, u32[]{:S(2)}, u32[]{:S(2)}) collective-permute-start(bf16[160,2048]{1,0:T(8,128)(2,1)S(1)} %slice.244), channel_id=1, source_target_pairs={{0,1},{1,0},{2,3},{3,2},{4,5},{5,4},{6,7},{7,6},{8,9},{9,8},{10,11... | collective-permute-start | bytes 1966088 | tf_op jit(solution)/shard_map/ppermute | solution.py:203
  196.2 14.0 %collective-permute-start.16 = (bf16[176,2048]{1,0:T(8,128)(2,1)S(1)}, bf16[176,2048]{1,0:T(8,128)(2,1)S(1)}, u32[]{:S(2)}, u32[]{:S(2)}) collective-permute-start(bf16[176,2048]{1,0:T(8,128)(2,1)S(1)} %slice.245), channel_id=1, source_target_pairs={{0,2},{1,3},{2,0},{3,1},{4,6},{5,7},{6,4},{7,5},{8,10},{9,11},{10,... | collective-permute-start | bytes 2162696 | tf_op jit(solution)/shard_map/ppermute | solution.py:203
  212.0 13.0 %collective-permute-start.17 = (bf16[160,2048]{1,0:T(8,128)(2,1)S(1)}, bf16[160,2048]{1,0:T(8,128)(2,1)S(1)}, u32[]{:S(2)}, u32[]{:S(2)}) collective-permute-start(bf16[160,2048]{1,0:T(8,128)(2,1)S(1)} %slice.189), channel_id=1, source_target_pairs={{0,1},{1,0},{2,3},{3,2},{4,5},{5,4},{6,7},{7,6},{8,9},{9,8},{10,11... | collective-permute-start | bytes 1966088 | tf_op jit(solution)/shard_map/ppermute | solution.py:203
  214.9 14.5 %collective-permute-start.18 = (bf16[176,2048]{1,0:T(8,128)(2,1)S(1)}, bf16[176,2048]{1,0:T(8,128)(2,1)S(1)}, u32[]{:S(2)}, u32[]{:S(2)}) collective-permute-start(bf16[176,2048]{1,0:T(8,128)(2,1)S(1)} %slice.190), channel_id=1, source_target_pairs={{0,2},{1,3},{2,0},{3,1},{4,6},{5,7},{6,4},{7,5},{8,10},{9,11},{10,... | collective-permute-start | bytes 2162696 | tf_op jit(solution)/shard_map/ppermute | solution.py:203
  271.8 209.3 %reduce-scatter.7.cloned.1.call-start = ((), (), s32[]{:S(2)}) async-start(), calls=%async_computation.9 | async-start | bytes 9437184 | tf_op jit(solution)/shard_map/reduce_scatter | solution.py:498
  296.8 19.2 %copy-start.41 = (bf16[1344,2048]{1,0:T(8,128)(2,1)S(1)}, bf16[1344,2048]{1,0:T(8,128)(2,1)}, u32[]{:S(2)}) copy-start(bf16[1344,2048]{1,0:T(8,128)(2,1)} %get-tuple-element.101) | copy-start | bytes 16515076
  303.9 12.1 %collective-permute-start.19 = (bf16[160,2048]{1,0:T(8,128)(2,1)S(1)}, bf16[160,2048]{1,0:T(8,128)(2,1)S(1)}, u32[]{:S(2)}, u32[]{:S(2)}) collective-permute-start(bf16[160,2048]{1,0:T(8,128)(2,1)S(1)} %slice.248), channel_id=1, source_target_pairs={{0,1},{1,0},{2,3},{3,2},{4,5},{5,4},{6,7},{7,6},{8,9},{9,8},{10,11... | collective-permute-start | bytes 1966088 | tf_op jit(solution)/shard_map/ppermute | solution.py:203
  304.9 21.6 %slice-start.4 = ((s8[8388608]{0:T(1024)(128)(4,1)}), s8[4194304]{0:T(1024)(128)(4,1)S(1)}, s32[]{:S(2)}) async-start(s8[8388608]{0:T(1024)(128)(4,1)} %bitcast.133), calls=%async_computation.16 | async-start | bytes 8388608
  305.0 21.6 %slice-start.5 = ((s8[8388608]{0:T(1024)(128)(4,1)}), s8[4194304]{0:T(1024)(128)(4,1)S(1)}, s32[]{:S(2)}) async-start(s8[8388608]{0:T(1024)(128)(4,1)} %bitcast.133), calls=%async_computation.17 | async-start | bytes 8388608
  305.0 21.6 %collective-permute-start.20 = (bf16[176,2048]{1,0:T(8,128)(2,1)S(1)}, bf16[176,2048]{1,0:T(8,128)(2,1)S(1)}, u32[]{:S(2)}, u32[]{:S(2)}) collective-permute-start(bf16[176,2048]{1,0:T(8,128)(2,1)S(1)} %slice.250), channel_id=1, source_target_pairs={{0,2},{1,3},{2,0},{3,1},{4,6},{5,7},{6,4},{7,5},{8,10},{9,11},{10,... | collective-permute-start | bytes 2162696 | tf_op jit(solution)/shard_map/ppermute | solution.py:203
  346.6 175.7 %reduce-scatter.11.cloned.1.call-start = ((), (), s32[]{:S(2)}) async-start(), calls=%async_computation.11 | async-start | bytes 2359296 | tf_op jit(solution)/shard_map/reduce_scatter | solution.py:514
  353.3 30.4 %copy-start.1 = (f32[336,2048]{1,0:T(8,128)S(1)}, f32[336,2048]{1,0:T(8,128)}, u32[]{:S(2)}) copy-start(f32[336,2048]{1,0:T(8,128)} %copy-done) | copy-start | bytes 8257540
  353.3 30.4 %copy-start.16 = (f32[2048]{0:T(1024)S(1)}, f32[2048]{0:T(1024)}, u32[]{:S(2)}) copy-start(f32[2048]{0:T(1024)} %param.28) | copy-start | bytes 24580
  353.3 30.4 %copy-start.23 = (f32[336]{0:T(512)S(1)}, f32[336]{0:T(512)}, u32[]{:S(2)}) copy-start(f32[336]{0:T(512)} %copy-done.22) | copy-start | bytes 4036
  353.3 30.4 %copy-start.28 = (f32[336]{0:T(512)S(1)}, f32[336]{0:T(512)}, u32[]{:S(2)}) copy-start(f32[336]{0:T(512)} %copy-done.27) | copy-start | bytes 4036
  353.3 28.9 %collective-permute-start.22 = (bf16[336,2048]{1,0:T(8,128)(2,1)S(1)}, bf16[336,2048]{1,0:T(8,128)(2,1)S(1)}, u32[]{:S(2)}, u32[]{:S(2)}) collective-permute-start(bf16[336,2048]{1,0:T(8,128)(2,1)S(1)} %copy-done.38), channel_id=1, source_target_pairs={{0,2},{1,3},{2,0},{3,1},{4,6},{5,7},{6,4},{7,5},{8,10},{9,11},{10,... | collective-permute-start | bytes 4128776 | tf_op jit(solution)/shard_map/ppermute | solution.py:203
  356.1 27.6 %collective-permute-start.21 = (bf16[336,2048]{1,0:T(8,128)(2,1)S(1)}, bf16[336,2048]{1,0:T(8,128)(2,1)S(1)}, u32[]{:S(2)}, u32[]{:S(2)}) collective-permute-start(bf16[336,2048]{1,0:T(8,128)(2,1)S(1)} %copy-done.39), channel_id=1, source_target_pairs={{0,1},{1,0},{2,3},{3,2},{4,5},{5,4},{6,7},{7,6},{8,9},{9,8},{10,11... | collective-permute-start | bytes 4128776 | tf_op jit(solution)/shard_map/ppermute | solution.py:203
  372.1 61.8 %copy-start.7 = (bf16[1344,2048]{1,0:T(8,128)(2,1)}, bf16[1344,2048]{1,0:T(8,128)(2,1)S(1)}, u32[]{:S(2)}) copy-start(bf16[1344,2048]{1,0:T(8,128)(2,1)S(1)} %convolution_convert_fusion) | copy-start | bytes 16515076
  388.4 29.7 %collective-permute-start.24 = (bf16[336,2048]{1,0:T(8,128)(2,1)S(1)}, bf16[336,2048]{1,0:T(8,128)(2,1)S(1)}, u32[]{:S(2)}, u32[]{:S(2)}) collective-permute-start(bf16[336,2048]{1,0:T(8,128)(2,1)S(1)} %get-tuple-element.78), channel_id=1, source_target_pairs={{0,2},{1,3},{2,0},{3,1},{4,6},{5,7},{6,4},{7,5},{8,10},{9,11},{10,... | collective-permute-start | bytes 4128776 | tf_op jit(solution)/shard_map/ppermute | solution.py:203
  388.8 30.5 %collective-permute-start.23 = (bf16[336,2048]{1,0:T(8,128)(2,1)S(1)}, bf16[336,2048]{1,0:T(8,128)(2,1)S(1)}, u32[]{:S(2)}, u32[]{:S(2)}) collective-permute-start(bf16[336,2048]{1,0:T(8,128)(2,1)S(1)} %get-tuple-element.78), channel_id=1, source_target_pairs={{0,1},{1,0},{2,3},{3,2},{4,5},{5,4},{6,7},{7,6},{8,9},{9,8},{10,11... | collective-permute-start | bytes 4128776 | tf_op jit(solution)/shard_map/ppermute | solution.py:203
  418.2 13.4 %collective-permute-start.25 = (bf16[160,2048]{1,0:T(8,128)(2,1)S(1)}, bf16[160,2048]{1,0:T(8,128)(2,1)S(1)}, u32[]{:S(2)}, u32[]{:S(2)}) collective-permute-start(bf16[160,2048]{1,0:T(8,128)(2,1)S(1)} %slice.252), channel_id=1, source_target_pairs={{0,1},{1,0},{2,3},{3,2},{4,5},{5,4},{6,7},{7,6},{8,9},{9,8},{10,11... | collective-permute-start | bytes 1966088 | tf_op jit(solution)/shard_map/ppermute | solution.py:203
  419.3 13.5 %collective-permute-start.26 = (bf16[176,2048]{1,0:T(8,128)(2,1)S(1)}, bf16[176,2048]{1,0:T(8,128)(2,1)S(1)}, u32[]{:S(2)}, u32[]{:S(2)}) collective-permute-start(bf16[176,2048]{1,0:T(8,128)(2,1)S(1)} %slice.253), channel_id=1, source_target_pairs={{0,2},{1,3},{2,0},{3,1},{4,6},{5,7},{6,4},{7,5},{8,10},{9,11},{10,... | collective-permute-start | bytes 2162696 | tf_op jit(solution)/shard_map/ppermute | solution.py:203
  433.9 16.9 %collective-permute-start.27 = (bf16[160,2048]{1,0:T(8,128)(2,1)}, bf16[160,2048]{1,0:T(8,128)(2,1)}, u32[]{:S(2)}, u32[]{:S(2)}) collective-permute-start(bf16[160,2048]{1,0:T(8,128)(2,1)} %slice.201), channel_id=1, source_target_pairs={{0,1},{1,0},{2,3},{3,2},{4,5},{5,4},{6,7},{7,6},{8,9},{9,8},{10,11... | collective-permute-start | bytes 1966088 | tf_op jit(solution)/shard_map/ppermute | solution.py:203
  434.7 16.1 %collective-permute-start.28 = (bf16[176,2048]{1,0:T(8,128)(2,1)S(1)}, bf16[176,2048]{1,0:T(8,128)(2,1)}, u32[]{:S(2)}, u32[]{:S(2)}) collective-permute-start(bf16[176,2048]{1,0:T(8,128)(2,1)S(1)} %slice.202), channel_id=1, source_target_pairs={{0,2},{1,3},{2,0},{3,1},{4,6},{5,7},{6,4},{7,5},{8,10},{9,11},{10,... | collective-permute-start | bytes 2162696 | tf_op jit(solution)/shard_map/ppermute | solution.py:203
  440.7 139.3 %reduce-scatter.9.cloned.1.call-start = ((), (), s32[]{:S(2)}) async-start(), calls=%async_computation.10 | async-start | bytes 3538944 | tf_op jit(solution)/shard_map/reduce_scatter | solution.py:523
  455.4 28.7 %collective-permute-start.30 = (bf16[336,2048]{1,0:T(8,128)(2,1)}, bf16[336,2048]{1,0:T(8,128)(2,1)}, u32[]{:S(2)}, u32[]{:S(2)}) collective-permute-start(bf16[336,2048]{1,0:T(8,128)(2,1)} %get-tuple-element.86), channel_id=1, source_target_pairs={{0,2},{1,3},{2,0},{3,1},{4,6},{5,7},{6,4},{7,5},{8,10},{9,11},{10,... | collective-permute-start | bytes 4128776 | tf_op jit(solution)/shard_map/ppermute | solution.py:203
  456.8 27.3 %collective-permute-start.29 = (bf16[336,2048]{1,0:T(8,128)(2,1)}, bf16[336,2048]{1,0:T(8,128)(2,1)}, u32[]{:S(2)}, u32[]{:S(2)}) collective-permute-start(bf16[336,2048]{1,0:T(8,128)(2,1)} %get-tuple-element.87), channel_id=1, source_target_pairs={{0,1},{1,0},{2,3},{3,2},{4,5},{5,4},{6,7},{7,6},{8,9},{9,8},{10,11... | collective-permute-start | bytes 4128776 | tf_op jit(solution)/shard_map/ppermute | solution.py:203
  501.0 10.7 %collective-permute-start.33 = (bf16[160,2048]{1,0:T(8,128)(2,1)S(1)}, bf16[160,2048]{1,0:T(8,128)(2,1)S(1)}, u32[]{:S(2)}, u32[]{:S(2)}) collective-permute-start(bf16[160,2048]{1,0:T(8,128)(2,1)S(1)} %slice.255), channel_id=1, source_target_pairs={{0,1},{1,0},{2,3},{3,2},{4,5},{5,4},{6,7},{7,6},{8,9},{9,8},{10,11... | collective-permute-start | bytes 1966088 | tf_op jit(solution)/shard_map/ppermute | solution.py:203
  502.5 15.6 %collective-permute-start.31 = (bf16[176,2048]{1,0:T(8,128)(2,1)S(1)}, bf16[176,2048]{1,0:T(8,128)(2,1)S(1)}, u32[]{:S(2)}, u32[]{:S(2)}) collective-permute-start(bf16[176,2048]{1,0:T(8,128)(2,1)S(1)} %slice.254), channel_id=1, source_target_pairs={{0,2},{1,3},{2,0},{3,1},{4,6},{5,7},{6,4},{7,5},{8,10},{9,11},{10,... | collective-permute-start | bytes 2162696 | tf_op jit(solution)/shard_map/ppermute | solution.py:203
  515.1 28.3 %collective-permute-start.34 = (bf16[336,2048]{1,0:T(8,128)(2,1)}, bf16[336,2048]{1,0:T(8,128)(2,1)S(1)}, u32[]{:S(2)}, u32[]{:S(2)}) collective-permute-start(bf16[336,2048]{1,0:T(8,128)(2,1)} %add_convert_fusion.2), channel_id=1, source_target_pairs={{0,2},{1,3},{2,0},{3,1},{4,6},{5,7},{6,4},{7,5},{8,10},{9,11},{10,... | collective-permute-start | bytes 4128776 | tf_op jit(solution)/shard_map/ppermute | solution.py:203
  521.5 22.2 %collective-permute-start.32 = (bf16[336,2048]{1,0:T(8,128)(2,1)}, bf16[336,2048]{1,0:T(8,128)(2,1)}, u32[]{:S(2)}, u32[]{:S(2)}) collective-permute-start(bf16[336,2048]{1,0:T(8,128)(2,1)} %add_convert_fusion.3), channel_id=1, source_target_pairs={{0,1},{1,0},{2,3},{3,2},{4,5},{5,4},{6,7},{7,6},{8,9},{9,8},{10,11... | collective-permute-start | bytes 4128776 | tf_op jit(solution)/shard_map/ppermute | solution.py:203
  526.7 17.0 %copy-start.3 = (bf16[336,2048]{1,0:T(8,128)(2,1)S(1)}, bf16[336,2048]{1,0:T(8,128)(2,1)}, u32[]{:S(2)}) copy-start(bf16[336,2048]{1,0:T(8,128)(2,1)} %param.17) | copy-start | bytes 4128772
  526.7 17.0 %copy-start.18 = (f32[2048]{0:T(1024)S(1)}, f32[2048]{0:T(1024)}, u32[]{:S(2)}) copy-start(f32[2048]{0:T(1024)} %param.20) | copy-start | bytes 24580
  526.7 17.0 %copy-start.21 = (f32[336]{0:T(512)S(1)}, f32[336]{0:T(512)}, u32[]{:S(2)}) copy-start(f32[336]{0:T(512)} %copy-done.20) | copy-start | bytes 4036
  526.7 17.0 %copy-start.26 = (f32[336]{0:T(512)S(1)}, f32[336]{0:T(512)}, u32[]{:S(2)}) copy-start(f32[336]{0:T(512)} %copy-done.25) | copy-start | bytes 4036
  581.6 5.4 collective-permute-start.36
  583.1 3.9 collective-permute-start.35
  583.7 4.8 collective-permute-start.37
  (31 other events, 182.0 us)
Sparse Core Ops, SparseCore 0:
  27.6 38.5 all-gather.4
  68.3 29.6 all-gather.6
  100.2 80.9 all-gather.8
  183.2 80.8 all-gather.10
  271.9 91.8 reduce-scatter.4
  366.0 87.9 reduce-scatter.6
  456.4 34.5 reduce-scatter.10
  496.9 49.6 reduce-scatter.8
